TPU v7x, 32 devices: a whole 2x2x4 slice. The times are simulated.
32 devices in a mesh: section: 4 (over y, x), dp: 8 (over z, core).
Axes of the slice: x: 2, y: 2, z: 4, core: 2. Of those that a mesh axis runs over, the one named last changes fastest.
Arguments:
- x_first: bfloat16 [4, 512, 4096], P('section', 'dp'), may hold values from -6 to 6
- x_second: bfloat16 [4, 512, 4096], P('section', 'dp'), may hold values from -6 to 6
- grad_first: bfloat16 [4, 512, 4096], P('section', 'dp'), may hold values from -6 to 6
- value_tiles: bfloat16 [4, 4, 16, 128, 128], P('section'), may hold values from -0.09375 to 0.09375
- output_tiles: bfloat16 [4, 4, 16, 128, 128], P('section'), may hold values from -0.125 to 0.125
- value_keep: int32 [4, 4, 16], P('section'), may hold values from 0 to 31, as said below
- output_keep: int32 [4, 4, 16], P('section'), may hold values from 0 to 31, as said below
Outputs:
- second_grad_in: bfloat16 [4, 512, 4096], P('section', 'dp')
- output_weight_grad: float32 [4, 64, 128, 128], P('section', 'dp')
Inputs may be any that keep to these rules, and one draw needn't show every extreme that they name: `value_keep`: each row [s, c] lists 16 distinct feature blocks in increasing order. `output_keep`: each row [s, c] lists 16 distinct feature blocks in increasing order.
All inputs are finite; a program needn't handle non-finite values.
Results may differ from a plain program's by a relative error of at most 0.005.
Values may be sent and summed in bfloat16 or wider, within the bound.
No kernel may reach another device: no remote copies, remote signals or barrier semaphores. Data moves between devices by JAX's collectives and lax.ppermute only.
A program may use at most 64 MiB of HBM per device.

v0:
```python
import jax
import jax.numpy as jnp
from jax import lax
from jax.sharding import PartitionSpec as P


def from_behind(value, axis, steps):
    count = lax.axis_size(axis)
    pairs = [(source, (source + steps) % count) for source in range(count)]
    return lax.ppermute(value, axis, pairs)


def layer_back(layer_in, upstream, w_value, w_output, value_idx, output_idx):
    tok_count = layer_in.shape[0]
    tile_size = w_value.shape[2]
    feat_blocks = layer_in.shape[1] // tile_size
    gathered_in = layer_in.reshape(tok_count, feat_blocks, tile_size)[:, value_idx]
    hidden_val = jnp.einsum(
        "tcjb,cjbk->tck", gathered_in, w_value, preferred_element_type=jnp.float32
    ).astype(jnp.bfloat16)
    up_blocks = upstream.reshape(tok_count, feat_blocks, tile_size)
    gathered_up = up_blocks[:, output_idx]
    hidden_grad = jnp.einsum(
        "tcjd,cjkd->tck", gathered_up, w_output, preferred_element_type=jnp.float32
    ).astype(jnp.bfloat16)
    partial_add = jnp.einsum(
        "tck,cjbk->tcjb", hidden_grad, w_value, preferred_element_type=jnp.float32
    )
    summed = up_blocks.astype(jnp.float32).at[:, value_idx].add(partial_add).reshape(tok_count, -1)
    return (summed.astype(jnp.bfloat16), hidden_val, gathered_up)


def per_device(x_first, x_second, grad_first, value_tiles, output_tiles, value_keep, output_keep):
    w_value = value_tiles[0]
    w_output = output_tiles[0]
    value_idx = value_keep[0]
    output_idx = output_keep[0]
    col_blocks = w_value.shape[0]
    kept_count = w_value.shape[1]
    tile_size = w_value.shape[2]
    total_tiles = col_blocks * kept_count
    first_in, first_hidden, first_up = layer_back(
        x_first[0], grad_first[0], w_value, w_output, value_idx, output_idx
    )
    arrived = from_behind(first_in, "section", -1)
    second_in, second_hidden, second_up = layer_back(
        x_second[0], arrived, w_value, w_output, value_idx, output_idx
    )
    scale = 1.0 / (2.0 * lax.axis_size("dp"))
    first_term = jnp.einsum(
        "tck,tcjd->cjkd", first_hidden, first_up, preferred_element_type=jnp.float32
    )
    second_term = jnp.einsum(
        "tck,tcjd->cjkd", second_hidden, second_up, preferred_element_type=jnp.float32
    )
    full_term = ((first_term + second_term) * scale).reshape(total_tiles, tile_size, tile_size)
    weight_grad = lax.psum_scatter(full_term, "dp", scatter_dimension=0, tiled=True)
    return (second_in[None], weight_grad[None])


def solution(mesh):
    in_specs = (
        P("section", "dp", None),
        P("section", "dp", None),
        P("section", "dp", None),
        P("section", None, None, None, None),
        P("section", None, None, None, None),
        P("section", None, None),
        P("section", None, None),
    )
    out_specs = (P("section", "dp", None), P("section", "dp", None, None))
    return jax.shard_map(
        per_device, mesh=mesh, in_specs=in_specs, out_specs=out_specs, check_vma=False
    )
```

profile of v0, /device:TPU:0, one launch (start us, length us, event | category | flops | bytes accessed | tf_op | source)
XLA Modules:
  0.0 117.4 jit_solution(455109684812871921)
XLA Ops:
  7.2 0.8 compare_select_fusion.1
  8.1 0.7 compare_select_fusion
  8.9 1.1 copy.36
  10.1 1.0 fusion.58
  11.1 2.7 %gather_fusion = bf16[64,64,128]{2,1,0:T(8,128)(2,1)} fusion(bf16[64,32,128]{2,0,1:T(8,128)(2,1)} %get-tuple-element.4, s32[1024]{0:T(1024)S(1)} %pad_clamp_fusion.1), kind=kCustom, calls=%fused_computation | custom fusion | bytes 2097408 | tf_op jit(solution)/shard_map/gather | solution.py:22
  13.8 4.8 %fusion.6 = f32[4,64,16,128]{3,1,2,0:T(8,128)} fusion(bf16[1,4,16,128,128]{4,3,2,1,0:T(8,128)(2,1)S(1)} %copy-done, bf16[64,4,16,128]{3,0,2,1:T(8,128)(2,1)} %bitcast.174, bf16[1,4,16,128,128]{4,3,2,1,0:T(8,128)(2,1)} %param.11), kind=kOutput, calls=%fused_computation.13 | convolution fusion | flops 268468224 | bytes 7340032 | tf_op jit(solution)/shard_map/tck,cjbk->tcjb/dot_general | solution.py:26
  18.6 7.0 %scatter_fusion = f32[64,32,128]{2,0,1:T(8,128)S(1)} fusion(f32[64,32,128]{2,0,1:T(8,128)S(1)} %get-tuple-element.5, s32[64]{0:T(128)S(1)} %reshape.116, f32[64,64,128]{2,1,0:T(8,128)} %bitcast.177), kind=kCustom, calls=%fused_computation.4 | custom fusion | flops 524288 | bytes 6291712 | tf_op jit(solution)/shard_map/scatter-add | solution.py:29
  25.6 0.9 copy_bitcast_fusion
  26.5 3.9 %collective-permute-start = (bf16[64,4096]{1,0:T(8,128)(2,1)}, bf16[64,4096]{1,0:T(8,128)(2,1)}, u32[]{:S(2)}, u32[]{:S(2)}) collective-permute-start(bf16[64,4096]{1,0:T(8,128)(2,1)} %copy_bitcast_fusion), channel_id=1, source_target_pairs={{0,24},{8,0},{16,8},{24,16},{1,25},{9,1},{17,9},{25,17},{2,26},{10... | collective-permute-start | bytes 1572872 | tf_op jit(solution)/shard_map/ppermute | solution.py:10
  30.4 1.1 copy.37
  31.6 1.0 copy.23
  32.7 1.0 copy.24
  33.7 2.8 %gather_fusion.2 = bf16[64,64,128]{2,1,0:T(8,128)(2,1)} fusion(bf16[64,32,128]{2,0,1:T(8,128)(2,1)} %copy.23, s32[1024]{0:T(1024)S(1)} %pad_clamp_fusion), kind=kCustom, calls=%fused_computation.2 | custom fusion | bytes 2097408 | tf_op jit(solution)/shard_map/gather | solution.py:17
  36.5 2.7 %gather_fusion.3 = bf16[64,64,128]{2,1,0:T(8,128)(2,1)} fusion(bf16[64,32,128]{2,0,1:T(8,128)(2,1)} %copy.24, s32[1024]{0:T(1024)S(1)} %pad_clamp_fusion), kind=kCustom, calls=%fused_computation.3 | custom fusion | bytes 2097408 | tf_op jit(solution)/shard_map/gather | solution.py:17
  39.2 4.4 %fusion.51 = f32[4,16,128,128]{3,2,1,0:T(8,128)} fusion(bf16[64,4,16,128]{3,0,2,1:T(8,128)(2,1)S(1)} %bitcast.175, bf16[64,4,16,128]{3,0,2,1:T(8,128)(2,1)} %bitcast.179, bf16[1,4,16,128,128]{4,3,2,1,0:T(8,128)(2,1)S(1)} %copy-done), kind=kOutput, calls=%fused_computation.31 | convolution fusion | flops 268468224 | bytes 8388608 | tf_op jit(solution)/shard_map/tck,tcjd->cjkd/dot_general | solution.py:50
  43.6 2.0 %copy_bitcast_fusion.1 = (bf16[64,32,128]{2,0,1:T(8,128)(2,1)}, f32[64,32,128]{2,0,1:T(8,128)S(1)}) fusion(bf16[64,4096]{1,0:T(8,128)(2,1)} %collective-permute-done), kind=kLoop, calls=%fused_computation.33 | loop fusion | flops 262144 | bytes 2097152 | tf_op jit(solution)/shard_map/reshape | solution.py:21
  45.6 2.8 %gather_fusion.1 = bf16[64,64,128]{2,1,0:T(8,128)(2,1)} fusion(bf16[64,32,128]{2,0,1:T(8,128)(2,1)} %get-tuple-element.2, s32[1024]{0:T(1024)S(1)} %pad_clamp_fusion.1), kind=kCustom, calls=%fused_computation.1 | custom fusion | bytes 2097408 | tf_op jit(solution)/shard_map/gather | solution.py:22
  48.4 6.0 %add_multiply_fusion = f32[4,16,128,128]{3,2,1,0:T(8,128)} fusion(f32[4,16,128,128]{3,2,1,0:T(8,128)} %fusion.51, bf16[64,4,16,128]{3,0,2,1:T(8,128)(2,1)} %bitcast.172, bf16[64,4,16,128]{3,0,2,1:T(8,128)(2,1)} %bitcast.178, bf16[1,4,16,128,128]{4,3,2,1,0:T(8,128)(2,1)S(1)} %copy-done), kind=kOutput, calls=%fused_computation.6 | convolution fusion | flops 270565376 | bytes 12582912 | tf_op jit(solution)/shard_map/tck,tcjd->cjkd/dot_general | solution.py:53
  54.4 5.6 %copy.25 = f32[64,128,128]{2,1,0:T(8,128)} copy(f32[64,128,128]{1,2,0:T(8,128)} %bitcast.171) | data formatting | bytes 8388608 | tf_op jit(solution)/shard_map/reshape | solution.py:56
  60.0 4.8 %fusion.4 = f32[4,64,16,128]{3,1,2,0:T(8,128)} fusion(bf16[1,4,16,128,128]{4,3,2,1,0:T(8,128)(2,1)S(1)} %copy-done, bf16[64,4,16,128]{3,0,2,1:T(8,128)(2,1)} %bitcast.173, bf16[1,4,16,128,128]{4,3,2,1,0:T(8,128)(2,1)} %param.11), kind=kOutput, calls=%fused_computation.11 | convolution fusion | flops 268468224 | bytes 7340032 | tf_op jit(solution)/shard_map/tck,cjbk->tcjb/dot_general | solution.py:26
  64.8 7.0 %scatter_fusion.1 = f32[64,32,128]{2,0,1:T(8,128)S(1)} fusion(f32[64,32,128]{2,0,1:T(8,128)S(1)} %get-tuple-element.3, s32[64]{0:T(128)S(1)} %reshape.116, f32[64,64,128]{2,1,0:T(8,128)} %bitcast.176), kind=kCustom, calls=%fused_computation.5 | custom fusion | flops 524288 | bytes 6291712 | tf_op jit(solution)/shard_map/scatter-add | solution.py:29
  71.9 0.3 copy.22
  72.2 1.0 convert_element_type.58
  73.3 37.3 %reduce-scatter.2.cloned.1.call-done = f32[8,128,128]{2,1,0:T(8,128)} async-done(((f32[64,128,128]{2,1,0:T(8,128)}), f32[8,128,128]{2,1,0:T(8,128)}) %reduce-scatter.2.cloned.1.call-update) | async-done | bytes 524304 | tf_op jit(solution)/shard_map/reduce_scatter | solution.py:57
  (15 shorter events, 0.4 us)
Async XLA Ops:
  7.2 6.6 %copy-start = (bf16[1,4,16,128,128]{4,3,2,1,0:T(8,128)(2,1)S(1)}, bf16[1,4,16,128,128]{4,3,2,1,0:T(8,128)(2,1)}, u32[]{:S(2)}) copy-start(bf16[1,4,16,128,128]{4,3,2,1,0:T(8,128)(2,1)} %param.10) | copy-start | bytes 6291460
  7.2 103.4 %reduce-scatter.2.cloned.1.call-start = ((), (), s32[]{:S(2)}) async-start(), calls=%async_computation.1 | async-start | bytes 4718592 | tf_op jit(solution)/shard_map/reduce_scatter | solution.py:57
  25.6 6.9 %copy-start.2 = (bf16[1,64,4096]{2,1,0:T(8,128)(2,1)S(1)}, bf16[1,64,4096]{2,1,0:T(8,128)(2,1)}, u32[]{:S(2)}) copy-start(bf16[1,64,4096]{2,1,0:T(8,128)(2,1)} %param.8) | copy-start | bytes 1572868
  26.5 17.1 %collective-permute-start = (bf16[64,4096]{1,0:T(8,128)(2,1)}, bf16[64,4096]{1,0:T(8,128)(2,1)}, u32[]{:S(2)}, u32[]{:S(2)}) collective-permute-start(bf16[64,4096]{1,0:T(8,128)(2,1)} %copy_bitcast_fusion), channel_id=1, source_target_pairs={{0,24},{8,0},{16,8},{24,16},{1,25},{9,1},{17,9},{25,17},{2,26},{10... | collective-permute-start | bytes 1572872 | tf_op jit(solution)/shard_map/ppermute | solution.py:10
  33.7 5.5 %copy-start.1 = (bf16[64,64,128]{2,1,0:T(8,128)(2,1)S(1)}, bf16[64,64,128]{2,1,0:T(8,128)(2,1)}, u32[]{:S(2)}) copy-start(bf16[64,64,128]{2,1,0:T(8,128)(2,1)} %gather_fusion) | copy-start | bytes 3145732
Sparse Core Ops, SparseCore 0:
  60.1 50.3 reduce-scatter.1
where the time goes:
time: 118 us; the launch traced here: 117 us
  waiting for transfers between devices  37.3 us (32%)
  local copies, waits for them, and re-layouts  22.6 us (19%)
  matrix products  19.9 us (17%)
  other arithmetic  19.5 us (17%)
  between operations  14.1 us (12%)
  starting transfers between devices  3.96 us (3%)
    reduce_scatter x1, waiting for transfers between devices, per_device(): lax.psum_scatter(full_term, 'dp', scatter_dimension=0, tiled=True)  37.3 us
    scatter-add x2, other arithmetic, layer_back(): up_blocks.astype(jnp.float32).at[:, value_idx].add(partial_add)  14 us
    dot_general x2, matrix products, layer_back(): jnp.einsum('tck,cjbk->tcjb', hidden_grad, w_value, preferred_element_type...  9.6 us
    dot_general x1, matrix products, per_device(): jnp.einsum('tck,tcjd->cjkd', second_hidden, second_up, preferred_element_...  5.97 us
    reshape x1, local copies, waits for them, and re-layouts, per_device(): ((first_term + second_term) * scale).reshape(total_tiles, tile_size, tile...  5.6 us
    gather x2, local copies, waits for them, and re-layouts, layer_back(): layer_in.reshape(tok_count, feat_blocks, tile_size)[:, value_idx]  5.54 us
    gather x2, local copies, waits for them, and re-layouts, layer_back(): gathered_up = up_blocks[:, output_idx]  5.5 us
    dot_general x1, matrix products, per_device(): jnp.einsum('tck,tcjd->cjkd', first_hidden, first_up, preferred_element_ty...  4.36 us
  transfers between devices with their start and end apart: 2, of which 1 were waited for; matrix products, arithmetic and copies ran while one was open for 22% of the time, Pallas kernels for 0%

commit v1 on v0

v1 whole, which is shorter than its diff:
```python
import functools

import jax
import jax.numpy as jnp
from jax import lax
from jax.experimental import pallas as pl
from jax.experimental.pallas import tpu as pltpu
from jax.sharding import PartitionSpec as P

F32 = jnp.float32
BF16 = jnp.bfloat16
NT = (((1,), (1,)), ((), ()))
NN = (((1,), (0,)), ((), ()))
VMEM = pl.BlockSpec(memory_space=pltpu.VMEM)
SMEM = pl.BlockSpec(memory_space=pltpu.SMEM)
HBM = pl.BlockSpec(memory_space=pl.ANY)


def block(ref, index, size):
    return ref[:, pl.ds(pl.multiple_of(index * size, size), size)]


def grad_kernel(parts_in, vk, ok, *refs):
    g_hbm = refs[:parts_in]
    o_hbm, v_hbm = refs[parts_in:parts_in + 2]
    outs = refs[parts_in + 2:-6]
    g_buf, o_buf, v_buf, acc, g_sem, w_sem = refs[-6:]
    kvb, keep, size, _ = o_buf.shape
    copies = []
    at = 0
    for i, part in enumerate(g_hbm):
        wide = part.shape[1]
        copies.append(pltpu.make_async_copy(part, g_buf.at[:, pl.ds(at, wide)], g_sem.at[i]))
        at += wide
    o_copies = [pltpu.make_async_copy(o_hbm.at[c], o_buf.at[c], w_sem.at[0, c]) for c in range(kvb)]
    v_copies = [pltpu.make_async_copy(v_hbm.at[c], v_buf.at[c], w_sem.at[1, c]) for c in range(kvb)]
    for copy in copies + o_copies + v_copies:
        copy.start()
    for copy in copies:
        copy.wait()
    hidden = []
    for c in range(kvb):
        o_copies[c].wait()
        total = None
        for j in range(0, keep, 2):
            left = jnp.concatenate([block(g_buf, ok[c, j + i], size) for i in (0, 1)], axis=1)
            right = jnp.concatenate([o_buf[c, j + i] for i in (0, 1)], axis=1)
            term = lax.dot_general(left, right, NT, preferred_element_type=F32)
            total = term if total is None else total + term
        hidden.append(total.astype(BF16))
    acc[...] = g_buf[...].astype(F32)
    for c in range(kvb):
        v_copies[c].wait()
        for j in range(keep):
            term = lax.dot_general(hidden[c], v_buf[c, j], NT, preferred_element_type=F32)
            cols = pl.ds(pl.multiple_of(vk[c, j] * size, size), size)
            acc[:, cols] = acc[:, cols] + term
    at = 0
    for out in outs:
        wide = out.shape[1]
        out[...] = acc[:, at:at + wide].astype(BF16)
        at += wide


def grad_call(g_parts, w_value, w_output, value_idx, output_idx, widths):
    tokens = g_parts[0].shape[0]
    width = sum(p.shape[1] for p in g_parts)
    kvb, keep, size, _ = w_value.shape
    flops = 4 * tokens * kvb * keep * size * size
    return pl.pallas_call(
        functools.partial(grad_kernel, len(g_parts)),
        out_shape=[jax.ShapeDtypeStruct((tokens, w), BF16) for w in widths],
        in_specs=[SMEM, SMEM] + [HBM] * (len(g_parts) + 2),
        out_specs=[VMEM] * len(widths),
        scratch_shapes=[
            pltpu.VMEM((tokens, width), BF16),
            pltpu.VMEM(w_output.shape, BF16),
            pltpu.VMEM(w_value.shape, BF16),
            pltpu.VMEM((tokens, width), F32),
            pltpu.SemaphoreType.DMA((len(g_parts),)),
            pltpu.SemaphoreType.DMA((2, kvb)),
        ],
        cost_estimate=pl.CostEstimate(flops=flops, bytes_accessed=6 << 20, transcendentals=0),
        name="grad",
    )(value_idx, output_idx, *g_parts, w_output, w_value)


def hidden_kernel(vk, x1_hbm, x2_hbm, v_hbm, out, x_buf, v_buf, x_sem, v_sem):
    tokens = x1_hbm.shape[0]
    kvb, keep, size, _ = v_buf.shape
    x_copies = [
        pltpu.make_async_copy(x1_hbm, x_buf.at[pl.ds(0, tokens)], x_sem.at[0]),
        pltpu.make_async_copy(x2_hbm, x_buf.at[pl.ds(tokens, tokens)], x_sem.at[1]),
    ]
    v_copies = [pltpu.make_async_copy(v_hbm.at[c], v_buf.at[c], v_sem.at[c]) for c in range(kvb)]
    for copy in x_copies + v_copies:
        copy.start()
    for copy in x_copies:
        copy.wait()
    for c in range(kvb):
        v_copies[c].wait()
        total = None
        for j in range(0, keep, 2):
            left = jnp.concatenate([block(x_buf, vk[c, j + i], size) for i in (0, 1)], axis=1)
            right = jnp.concatenate([v_buf[c, j + i] for i in (0, 1)], axis=0)
            term = lax.dot_general(left, right, NN, preferred_element_type=F32)
            total = term if total is None else total + term
        out[c] = total.astype(BF16).T


def hidden_call(x1, x2, w_value, value_idx):
    tokens, width = x1.shape
    kvb, keep, size, _ = w_value.shape
    return pl.pallas_call(
        hidden_kernel,
        out_shape=jax.ShapeDtypeStruct((kvb, size, 2 * tokens), BF16),
        in_specs=[SMEM, HBM, HBM, HBM],
        out_specs=VMEM,
        scratch_shapes=[
            pltpu.VMEM((2 * tokens, width), BF16),
            pltpu.VMEM(w_value.shape, BF16),
            pltpu.SemaphoreType.DMA((2,)),
            pltpu.SemaphoreType.DMA((kvb,)),
        ],
        cost_estimate=pl.CostEstimate(
            flops=4 * tokens * kvb * keep * size * size, bytes_accessed=4 << 20, transcendentals=0
        ),
        name="hidden",
    )(value_idx, x1, x2, w_value)


def reverse_bits(value, bits):
    out = 0
    for _ in range(bits):
        out, value = out * 2 + value % 2, value // 2
    return out


def tile_kernel(per, bits, me, ok, h_ref, g_ref, *refs):
    arrived, outs, stack = refs[:-5], refs[-5:-1], refs[-1]
    tokens = g_ref.shape[0]
    size = h_ref.shape[1]
    keep = ok.shape[1]
    stack[:tokens] = g_ref[...]
    at = 0
    for part in arrived:
        wide = part.shape[1]
        stack[tokens:, at:at + wide] = part[...]
        at += wide
    flip = me[0] * per
    position = (2 ** bits) * per - 1
    for out in outs:
        for i in reversed(range(out.shape[0])):
            tile = (reverse_bits(position // per, bits) * per + position % per) ^ flip
            c, j = tile // keep, lax.rem(tile, keep)
            term = lax.dot_general(
                h_ref[c], block(stack, ok[c, j], size), NN, preferred_element_type=F32
            )
            out[i] = term.astype(out.dtype)
            position -= 1


def tile_call(me, output_idx, hidden, g, arrived, ranks):
    kvb, size, stacked = hidden.shape
    keep = output_idx.shape[1]
    total = kvb * keep
    bits = ranks.bit_length() - 1
    per = total // ranks
    sizes = [(total // 4, BF16), (total // 4, BF16), (total // 4, F32), (total // 4, F32)]
    return pl.pallas_call(
        functools.partial(tile_kernel, per, bits),
        out_shape=[jax.ShapeDtypeStruct((n, size, size), t) for n, t in sizes],
        in_specs=[SMEM, SMEM] + [VMEM] * (2 + len(arrived)),
        out_specs=[VMEM] * 4,
        scratch_shapes=[pltpu.VMEM((stacked, g.shape[1]), BF16)],
        cost_estimate=pl.CostEstimate(
            flops=2 * stacked * total * size * size, bytes_accessed=4 << 20, transcendentals=0
        ),
        name="tiles",
    )(me, output_idx, hidden, g, *arrived)


def exchange(value, axis, bit):
    count = lax.axis_size(axis)
    return lax.ppermute(value, axis, [(i, i ^ bit) for i in range(count)])


def from_behind(value, axis, steps):
    count = lax.axis_size(axis)
    return lax.ppermute(value, axis, [(i, (i + steps) % count) for i in range(count)])


def per_device(x_first, x_second, grad_first, value_tiles, output_tiles, value_keep, output_keep):
    w_value, w_output = value_tiles[0], output_tiles[0]
    value_idx, output_idx = value_keep[0], output_keep[0]
    g = grad_first[0]
    width = g.shape[1]
    ranks = lax.axis_size("dp")
    me = lax.axis_index("dp").astype(jnp.int32).reshape(1)
    parts = 4
    widths = [width // parts] * parts
    first = grad_call([g], w_value, w_output, value_idx, output_idx, widths)
    arrived = [from_behind(p, "section", -1) for p in first]
    hidden = hidden_call(x_first[0], x_second[0], w_value, value_idx)
    send_near, send_far, keep_far, keep_near = tile_call(me, output_idx, hidden, g, arrived, ranks)
    got_near = exchange(send_near, "dp", 1)
    got_far = exchange(send_far, "dp", 1)
    (second,) = grad_call(arrived, w_value, w_output, value_idx, output_idx, [width])
    leaving = keep_far + got_near.astype(F32)
    staying = keep_near + got_far.astype(F32)
    bit = 2
    while bit < ranks:
        came = exchange(leaving.astype(BF16), "dp", bit).astype(F32)
        bit *= 2
        staying = staying + came
        half = staying.shape[0] // 2
        if bit < ranks:
            staying, leaving = staying[:half], staying[half:]
    weight_grad = staying * (1.0 / (2.0 * ranks))
    return second[None], weight_grad[None]


def solution(mesh):
    in_specs = (
        P("section", "dp", None),
        P("section", "dp", None),
        P("section", "dp", None),
        P("section", None, None, None, None),
        P("section", None, None, None, None),
        P("section", None, None),
        P("section", None, None),
    )
    out_specs = (P("section", "dp", None), P("section", "dp", None, None))
    return jax.shard_map(
        per_device, mesh=mesh, in_specs=in_specs, out_specs=out_specs, check_vma=False
    )
```

time: 118 us -> 60.7 us (0.51)
  Pallas kernels: 0 us -> 22.8 us
  local copies, waits for them, and re-layouts: 22.6 us -> 0.7 us
  matrix products: 19.9 us -> 0 us
  other arithmetic: 19.5 us -> 2.38 us
  waiting for transfers between devices: 37.3 us -> 23 us
  between operations: 14.1 us -> 0.71 us
  starting transfers between devices: 3.96 us -> 10.8 us
    reduce_scatter x1 -> x0, waiting for transfers between devices: 37.3 us -> none  [per_device(): lax.psum_scatter(full_term, 'dp', scatter_dimension=0, tiled=True)]
    ppermute x1 -> x8, waiting for transfers between devices: 0.01 us -> 23 us  [the longest x4 18.1 us: exchange(): return lax.ppermute(value, axis, [(i, i ^ bit) for i in range(count)])]
    pallas_call x0 -> x4, Pallas kernels: none -> 22.8 us  [the longest x2 14.6 us: grad_call(): pl.pallas_call(functools.partial(grad_kernel, len(g_parts)), out_shape=[j...]
    dot_general x4 -> x0, matrix products: 19.9 us -> none  [the longest x2 9.6 us: layer_back(): jnp.einsum('tck,cjbk->tcjb', hidden_grad, w_value, preferred_element_type...]
    scatter-add x2 -> x0, other arithmetic: 14 us -> none  [layer_back(): up_blocks.astype(jnp.float32).at[:, value_idx].add(partial_add)]
    gather x4 -> x0, local copies, waits for them, and re-layouts: 11 us -> none  [the longest x2 5.54 us: layer_back(): layer_in.reshape(tok_count, feat_blocks, tile_size)[:, value_idx]]
    ppermute x1 -> x8, starting transfers between devices: 3.93 us -> 10.8 us  [the longest x4 6.01 us: from_behind(): lax.ppermute(value, axis, [(i, (i + steps) % count) for i in range(count)])]
    reshape x1 -> x0, local copies, waits for them, and re-layouts: 5.6 us -> none  [per_device(): ((first_term + second_term) * scale).reshape(total_tiles, tile_size, tile...]
  transfers between devices with their start and end apart: 2 -> 8, of which waited for: 1 -> 6; matrix products, arithmetic and copies ran while one was open for 22% -> 2% of each run, Pallas kernels for 0% -> 20%
where the time goes in v1:
time: 60.7 us; the launch traced here: 60.4 us
  waiting for transfers between devices  23 us (38%)
  Pallas kernels  22.8 us (38%)
  starting transfers between devices  10.8 us (18%)
  other arithmetic  2.38 us (4%)
  between operations  0.71 us (1%)
  local copies, waits for them, and re-layouts  0.7 us (1%)
    ppermute x4, waiting for transfers between devices, exchange(): return lax.ppermute(value, axis, [(i, i ^ bit) for i in range(count)])  18.1 us
    pallas_call x2, Pallas kernels, grad_call(): pl.pallas_call(functools.partial(grad_kernel, len(g_parts)), out_shape=[j...  14.6 us
    ppermute x4, starting transfers between devices, from_behind(): lax.ppermute(value, axis, [(i, (i + steps) % count) for i in range(count)])  6.01 us
    ppermute x4, waiting for transfers between devices, from_behind(): lax.ppermute(value, axis, [(i, (i + steps) % count) for i in range(count)])  4.95 us
    ppermute x4, starting transfers between devices, exchange(): return lax.ppermute(value, axis, [(i, i ^ bit) for i in range(count)])  4.81 us
    pallas_call x1, Pallas kernels, hidden_call(): pl.pallas_call(hidden_kernel, out_shape=jax.ShapeDtypeStruct((kvb, size,...  4.49 us
    pallas_call x1, Pallas kernels, tile_call(): pl.pallas_call(functools.partial(tile_kernel, per, bits), out_shape=[jax....  3.66 us
    convert_element_type x1, other arithmetic, per_device(): came = exchange(leaving.astype(BF16), 'dp', bit).astype(F32)  1.36 us
  transfers between devices with their start and end apart: 8, of which 6 were waited for; matrix products, arithmetic and copies ran while one was open for 2% of the time, Pallas kernels for 20%

profile of v1, /device:TPU:0, one launch (start us, length us, event | category | flops | bytes accessed | tf_op | source)
XLA Modules:
  0.0 60.4 jit_solution(2803806354351223029)
XLA Ops:
  0.6 7.3 %grad.2 = (bf16[64,1024]{1,0:T(8,128)(2,1)}, bf16[64,1024]{1,0:T(8,128)(2,1)}, bf16[64,1024]{1,0:T(8,128)(2,1)}, bf16[64,1024]{1,0:T(8,128)(2,1)}) custom-call(s32[4,16]{1,0:T(4,128)} %bitcast.24, s32[4,16]{1,0:T(4,128)} %bitcast.21, bf16[64,4096]{1,0:T(8,128)(2,1)} %bitcast.16, bf16[4,16,128,128]{3,2,1,0:T(8,128)(2,1)} %bitcast.14, ...), custom_call_target="tpu_custom_call" | custom-call | flops 268435456 | bytes 6291456 | tf_op jit(solution)/shard_map/grad/pallas_call | solution.py:70
  7.9 4.0 %collective-permute-start = (bf16[64,1024]{1,0:T(8,128)(2,1)}, bf16[64,1024]{1,0:T(8,128)(2,1)S(1)}, u32[]{:S(2)}, u32[]{:S(2)}) collective-permute-start(bf16[64,1024]{1,0:T(8,128)(2,1)} %get-tuple-element.10), channel_id=1, source_target_pairs={{0,24},{8,0},{16,8},{24,16},{1,25},{9,1},{17,9},{25,17},{2,26},{10... | collective-permute-start | bytes 393224 | tf_op jit(solution)/shard_map/ppermute | solution.py:190
  11.9 0.5 collective-permute-start.1
  12.4 1.4 %collective-permute-start.2 = (bf16[64,1024]{1,0:T(8,128)(2,1)}, bf16[64,1024]{1,0:T(8,128)(2,1)S(1)}, u32[]{:S(2)}, u32[]{:S(2)}) collective-permute-start(bf16[64,1024]{1,0:T(8,128)(2,1)} %get-tuple-element.12), channel_id=1, source_target_pairs={{0,24},{8,0},{16,8},{24,16},{1,25},{9,1},{17,9},{25,17},{2,26},{10... | collective-permute-start | bytes 393224 | tf_op jit(solution)/shard_map/ppermute | solution.py:190
  13.9 0.1 collective-permute-start.3
  13.9 4.5 %hidden.1.h_ref = bf16[4,128,128]{2,1,0:T(8,128)(2,1)} custom-call(s32[4,16]{1,0:T(4,128)} %bitcast.25, bf16[64,4096]{1,0:T(8,128)(2,1)} %bitcast.19, bf16[64,4096]{1,0:T(8,128)(2,1)} %bitcast.20, bf16[4,16,128,128]{3,2,1,0:T(8,128)(2,1)} %bitcast.12), custom_call_target="tpu_custom_call" | custom-call | flops 268435456 | bytes 4194304 | tf_op jit(solution)/shard_map/hidden/pallas_call | solution.py:114
  18.4 0.0 collective-permute-done.refs_0_
  18.5 0.5 collective-permute-done.1.refs_1_
  18.9 2.8 %collective-permute-done.2.refs_2_ = bf16[64,1024]{1,0:T(8,128)(2,1)S(1)} collective-permute-done((bf16[64,1024]{1,0:T(8,128)(2,1)}, bf16[64,1024]{1,0:T(8,128)(2,1)S(1)}, u32[]{:S(2)}, u32[]{:S(2)}) %collective-permute-start.2) | collective-permute-done | bytes 131104 | tf_op jit(solution)/shard_map/ppermute | solution.py:190
  21.7 1.7 %collective-permute-done.3.refs_3_ = bf16[64,1024]{1,0:T(8,128)(2,1)S(1)} collective-permute-done((bf16[64,1024]{1,0:T(8,128)(2,1)}, bf16[64,1024]{1,0:T(8,128)(2,1)S(1)}, u32[]{:S(2)}, u32[]{:S(2)}) %collective-permute-start.3) | collective-permute-done | bytes 131104 | tf_op jit(solution)/shard_map/ppermute | solution.py:190
  23.4 0.6 %copy-done.4 = bf16[64,1024]{1,0:T(8,128)(2,1)} copy-done((bf16[64,1024]{1,0:T(8,128)(2,1)}, bf16[64,1024]{1,0:T(8,128)(2,1)S(1)}, u32[]{:S(2)}) %copy-start.4) | copy-done | bytes 131096
  24.1 3.7 %tiles.1 = (bf16[16,128,128]{2,1,0:T(8,128)(2,1)}, bf16[16,128,128]{2,1,0:T(8,128)(2,1)}, f32[16,128,128]{2,1,0:T(8,128)}, f32[16,128,128]{2,1,0:T(8,128)}) custom-call(s32[1]{0:T(128)} %bitcast.6.me, s32[4,16]{1,0:T(4,128)} %bitcast.22, bf16[4,128,128]{2,1,0:T(8,128)(2,1)} %hidden.1.h_ref, bf16[64,4096]{1,0:T(8,128)(2,1)} %bitcast.17, ...), custom_call_target="tpu_custom_call" | custom-call | flops 268435456 | bytes 4194304 | tf_op jit(solution)/shard_map/tiles/pallas_call | solution.py:170
  27.7 0.0 collective-permute-start.5
  27.7 0.5 collective-permute-start.4
  28.2 1.6 %collective-permute-done.5 = bf16[16,128,128]{2,1,0:T(8,128)(2,1)S(1)} collective-permute-done((bf16[16,128,128]{2,1,0:T(8,128)(2,1)}, bf16[16,128,128]{2,1,0:T(8,128)(2,1)S(1)}, u32[]{:S(2)}, u32[]{:S(2)}) %collective-permute-start.5) | collective-permute-done | bytes 524320 | tf_op jit(solution)/shard_map/ppermute | solution.py:185
  29.9 1.4 %add_convert_fusion = bf16[16,128,128]{2,1,0:T(8,128)(2,1)S(1)} fusion(f32[16,128,128]{2,1,0:T(8,128)} %get-tuple-element.16, bf16[16,128,128]{2,1,0:T(8,128)(2,1)S(1)} %collective-permute-done.5), kind=kLoop, calls=%fused_computation.1 | loop fusion | flops 786432 | bytes 2097152 | tf_op jit(solution)/shard_map/convert_element_type | solution.py:213
  31.2 1.6 %collective-permute-start.6 = (bf16[16,128,128]{2,1,0:T(8,128)(2,1)S(1)}, bf16[16,128,128]{2,1,0:T(8,128)(2,1)S(1)}, u32[]{:S(2)}, u32[]{:S(2)}) collective-permute-start(bf16[16,128,128]{2,1,0:T(8,128)(2,1)S(1)} %add_convert_fusion), channel_id=1, source_target_pairs={{0,2},{1,3},{2,0},{3,1},{4,6},{5,7},{6,4},{7,5},{8,10},{9,11},{10,... | collective-permute-start | bytes 1572872 | tf_op jit(solution)/shard_map/ppermute | solution.py:185
  32.9 0.0 collective-permute-done.4
  32.9 12.4 %collective-permute-done.6 = bf16[16,128,128]{2,1,0:T(8,128)(2,1)S(1)} collective-permute-done((bf16[16,128,128]{2,1,0:T(8,128)(2,1)S(1)}, bf16[16,128,128]{2,1,0:T(8,128)(2,1)S(1)}, u32[]{:S(2)}, u32[]{:S(2)}) %collective-permute-start.6) | collective-permute-done | bytes 524320 | tf_op jit(solution)/shard_map/ppermute | solution.py:185
  45.2 0.2 convert_add_fusion
  45.5 2.7 %collective-permute-start.7 = (bf16[8,128,128]{2,1,0:T(8,128)(2,1)S(1)}, bf16[8,128,128]{2,1,0:T(8,128)(2,1)S(1)}, u32[]{:S(2)}, u32[]{:S(2)}) collective-permute-start(bf16[8,128,128]{2,1,0:T(8,128)(2,1)S(1)} %slice.17), channel_id=1, source_target_pairs={{0,4},{1,5},{2,6},{3,7},{4,0},{5,1},{6,2},{7,3},{8,12},{9,13},{10,... | collective-permute-start | bytes 786440 | tf_op jit(solution)/shard_map/ppermute | solution.py:185
  48.1 7.3 %grad.3 = bf16[64,4096]{1,0:T(8,128)(2,1)} custom-call(s32[4,16]{1,0:T(4,128)} %bitcast.26, s32[4,16]{1,0:T(4,128)} %bitcast.23, bf16[64,1024]{1,0:T(8,128)(2,1)} %copy-done.1, bf16[64,1024]{1,0:T(8,128)(2,1)} %copy-done.2, bf16[64,1024]{1,0:T(8,128)(2,1)} %copy-done.3, bf16[64,1024]{1,0:T(8,128)(2,1)} %copy-done.4, bf16[4,16,128,128]{3,2,1,0:T(8,128)(2,1)} %bitcast.15, ...), custom_call_target="tpu_custom_call" | custom-call | flops 268435456 | bytes 6291456 | tf_op jit(solution)/shard_map/grad/pallas_call | solution.py:70
  55.5 4.1 %collective-permute-done.7 = bf16[8,128,128]{2,1,0:T(8,128)(2,1)S(1)} collective-permute-done((bf16[8,128,128]{2,1,0:T(8,128)(2,1)S(1)}, bf16[8,128,128]{2,1,0:T(8,128)(2,1)S(1)}, u32[]{:S(2)}, u32[]{:S(2)}) %collective-permute-start.7) | collective-permute-done | bytes 262176 | tf_op jit(solution)/shard_map/ppermute | solution.py:185
  59.5 0.8 %fusion.1 = f32[1,8,128,128]{3,2,1,0:T(8,128)} fusion(f32[16,128,128]{2,1,0:T(8,128)S(1)} %convert_add_fusion, bf16[8,128,128]{2,1,0:T(8,128)(2,1)S(1)} %collective-permute-done.7), kind=kLoop, calls=%fused_computation.5 | loop fusion | flops 393216 | bytes 1310720 | tf_op jit(solution)/shard_map/broadcast_in_dim | solution.py:220
  (10 shorter events, 0.1 us)
Async XLA Ops:
  7.9 10.5 %collective-permute-start = (bf16[64,1024]{1,0:T(8,128)(2,1)}, bf16[64,1024]{1,0:T(8,128)(2,1)S(1)}, u32[]{:S(2)}, u32[]{:S(2)}) collective-permute-start(bf16[64,1024]{1,0:T(8,128)(2,1)} %get-tuple-element.10), channel_id=1, source_target_pairs={{0,24},{8,0},{16,8},{24,16},{1,25},{9,1},{17,9},{25,17},{2,26},{10... | collective-permute-start | bytes 393224 | tf_op jit(solution)/shard_map/ppermute | solution.py:190
  11.9 7.0 %collective-permute-start.1 = (bf16[64,1024]{1,0:T(8,128)(2,1)}, bf16[64,1024]{1,0:T(8,128)(2,1)S(1)}, u32[]{:S(2)}, u32[]{:S(2)}) collective-permute-start(bf16[64,1024]{1,0:T(8,128)(2,1)} %get-tuple-element.11), channel_id=1, source_target_pairs={{0,24},{8,0},{16,8},{24,16},{1,25},{9,1},{17,9},{25,17},{2,26},{10... | collective-permute-start | bytes 393224 | tf_op jit(solution)/shard_map/ppermute | solution.py:190
  12.4 9.3 %collective-permute-start.2 = (bf16[64,1024]{1,0:T(8,128)(2,1)}, bf16[64,1024]{1,0:T(8,128)(2,1)S(1)}, u32[]{:S(2)}, u32[]{:S(2)}) collective-permute-start(bf16[64,1024]{1,0:T(8,128)(2,1)} %get-tuple-element.12), channel_id=1, source_target_pairs={{0,24},{8,0},{16,8},{24,16},{1,25},{9,1},{17,9},{25,17},{2,26},{10... | collective-permute-start | bytes 393224 | tf_op jit(solution)/shard_map/ppermute | solution.py:190
  13.9 9.5 %collective-permute-start.3 = (bf16[64,1024]{1,0:T(8,128)(2,1)}, bf16[64,1024]{1,0:T(8,128)(2,1)S(1)}, u32[]{:S(2)}, u32[]{:S(2)}) collective-permute-start(bf16[64,1024]{1,0:T(8,128)(2,1)} %get-tuple-element.13), channel_id=1, source_target_pairs={{0,24},{8,0},{16,8},{24,16},{1,25},{9,1},{17,9},{25,17},{2,26},{10... | collective-permute-start | bytes 393224 | tf_op jit(solution)/shard_map/ppermute | solution.py:190
  18.4 5.0 %copy-start.1 = (bf16[64,1024]{1,0:T(8,128)(2,1)}, bf16[64,1024]{1,0:T(8,128)(2,1)S(1)}, u32[]{:S(2)}) copy-start(bf16[64,1024]{1,0:T(8,128)(2,1)S(1)} %collective-permute-done.refs_0_) | copy-start | bytes 393220
  18.9 4.5 %copy-start.2 = (bf16[64,1024]{1,0:T(8,128)(2,1)}, bf16[64,1024]{1,0:T(8,128)(2,1)S(1)}, u32[]{:S(2)}) copy-start(bf16[64,1024]{1,0:T(8,128)(2,1)S(1)} %collective-permute-done.1.refs_1_) | copy-start | bytes 393220
  21.7 1.7 %copy-start.3 = (bf16[64,1024]{1,0:T(8,128)(2,1)}, bf16[64,1024]{1,0:T(8,128)(2,1)S(1)}, u32[]{:S(2)}) copy-start(bf16[64,1024]{1,0:T(8,128)(2,1)S(1)} %collective-permute-done.2.refs_2_) | copy-start | bytes 393220
  23.4 0.7 %copy-start.4 = (bf16[64,1024]{1,0:T(8,128)(2,1)}, bf16[64,1024]{1,0:T(8,128)(2,1)S(1)}, u32[]{:S(2)}) copy-start(bf16[64,1024]{1,0:T(8,128)(2,1)S(1)} %collective-permute-done.3.refs_3_) | copy-start | bytes 393220
  27.7 17.5 %copy-start = (f32[16,128,128]{2,1,0:T(8,128)S(1)}, f32[16,128,128]{2,1,0:T(8,128)}, u32[]{:S(2)}) copy-start(f32[16,128,128]{2,1,0:T(8,128)} %get-tuple-element.14) | copy-start | bytes 3145732
  27.7 2.1 %collective-permute-start.5 = (bf16[16,128,128]{2,1,0:T(8,128)(2,1)}, bf16[16,128,128]{2,1,0:T(8,128)(2,1)S(1)}, u32[]{:S(2)}, u32[]{:S(2)}) collective-permute-start(bf16[16,128,128]{2,1,0:T(8,128)(2,1)} %get-tuple-element.17), channel_id=1, source_target_pairs={{0,1},{1,0},{2,3},{3,2},{4,5},{5,4},{6,7},{7,6},{8,9},{9,8},{10,11... | collective-permute-start | bytes 1572872 | tf_op jit(solution)/shard_map/ppermute | solution.py:185
  27.7 5.1 %collective-permute-start.4 = (bf16[16,128,128]{2,1,0:T(8,128)(2,1)}, bf16[16,128,128]{2,1,0:T(8,128)(2,1)S(1)}, u32[]{:S(2)}, u32[]{:S(2)}) collective-permute-start(bf16[16,128,128]{2,1,0:T(8,128)(2,1)} %get-tuple-element.15), channel_id=1, source_target_pairs={{0,1},{1,0},{2,3},{3,2},{4,5},{5,4},{6,7},{7,6},{8,9},{9,8},{10,11... | collective-permute-start | bytes 1572872 | tf_op jit(solution)/shard_map/ppermute | solution.py:185
  31.2 14.0 %collective-permute-start.6 = (bf16[16,128,128]{2,1,0:T(8,128)(2,1)S(1)}, bf16[16,128,128]{2,1,0:T(8,128)(2,1)S(1)}, u32[]{:S(2)}, u32[]{:S(2)}) collective-permute-start(bf16[16,128,128]{2,1,0:T(8,128)(2,1)S(1)} %add_convert_fusion), channel_id=1, source_target_pairs={{0,2},{1,3},{2,0},{3,1},{4,6},{5,7},{6,4},{7,5},{8,10},{9,11},{10,... | collective-permute-start | bytes 1572872 | tf_op jit(solution)/shard_map/ppermute | solution.py:185
  45.5 14.1 %collective-permute-start.7 = (bf16[8,128,128]{2,1,0:T(8,128)(2,1)S(1)}, bf16[8,128,128]{2,1,0:T(8,128)(2,1)S(1)}, u32[]{:S(2)}, u32[]{:S(2)}) collective-permute-start(bf16[8,128,128]{2,1,0:T(8,128)(2,1)S(1)} %slice.17), channel_id=1, source_target_pairs={{0,4},{1,5},{2,6},{3,7},{4,0},{5,1},{6,2},{7,3},{8,12},{9,13},{10,... | collective-permute-start | bytes 786440 | tf_op jit(solution)/shard_map/ppermute | solution.py:185

commit v2 on v1

v2 whole, which is shorter than its diff:
```python
import functools

import jax
import jax.numpy as jnp
from jax import lax
from jax.experimental import pallas as pl
from jax.experimental.pallas import tpu as pltpu
from jax.sharding import PartitionSpec as P

F32 = jnp.float32
BF16 = jnp.bfloat16
NT = (((1,), (1,)), ((), ()))
NN = (((1,), (0,)), ((), ()))
VMEM = pl.BlockSpec(memory_space=pltpu.VMEM)
SMEM = pl.BlockSpec(memory_space=pltpu.SMEM)
HBM = pl.BlockSpec(memory_space=pl.ANY)
ROOM = pltpu.CompilerParams(vmem_limit_bytes=16 << 20)


def cost(flops, nbytes):
    return pl.CostEstimate(flops=flops, bytes_accessed=nbytes, transcendentals=0)


def block(ref, index, size):
    return ref[:, pl.ds(pl.multiple_of(index * size, size), size)]


def pairs(keep):
    return [(j, j + 1) for j in range(0, keep, 2)]


def hidden_grad(ok, g, o, c):
    keep, size = o.shape[1], o.shape[2]
    total = None
    for both in pairs(keep):
        left = jnp.concatenate([block(g, ok[c, j], size) for j in both], axis=1)
        right = jnp.concatenate([o[c, j] for j in both], axis=1)
        term = lax.dot_general(left, right, NT, preferred_element_type=F32)
        total = term if total is None else total + term
    return total.astype(BF16)


def add_back(vk, hidden, v, c, acc):
    keep, size = v.shape[1], v.shape[2]
    for both in pairs(keep):
        right = jnp.concatenate([v[c, j] for j in both], axis=0)
        term = lax.dot_general(hidden, right, NT, preferred_element_type=F32)
        for i, j in enumerate(both):
            cols = pl.ds(pl.multiple_of(vk[c, j] * size, size), size)
            acc[:, cols] = acc[:, cols] + term[:, i * size:(i + 1) * size]


def write_parts(acc, outs):
    at = 0
    for out in outs:
        wide = out.shape[1]
        out[...] = acc[:, at:at + wide].astype(BF16)
        at += wide


def first_kernel(vk_hbm, ok_hbm, g_hbm, o_hbm, v_hbm, *refs):
    outs, (g, o, v, acc, vk, ok, sem, w_sem) = refs[:-8], refs[-8:]
    kvb = o.shape[0]
    copy = pltpu.make_async_copy
    small = [copy(ok_hbm, ok, sem.at[0]), copy(g_hbm, g, sem.at[1]), copy(vk_hbm, vk, sem.at[2])]
    o_copies = [copy(o_hbm.at[c], o.at[c], w_sem.at[0, c]) for c in range(kvb)]
    v_copies = [copy(v_hbm.at[c], v.at[c], w_sem.at[1, c]) for c in range(kvb)]
    for each in small + o_copies + v_copies:
        each.start()
    small[0].wait()
    small[1].wait()
    acc[...] = g[...].astype(F32)
    hidden = []
    for c in range(kvb):
        o_copies[c].wait()
        hidden.append(hidden_grad(ok, g, o, c))
    small[2].wait()
    for c in range(kvb):
        v_copies[c].wait()
        add_back(vk, hidden[c], v, c, acc)
    write_parts(acc, outs)


def first_call(g, w_value, w_output, value_idx, output_idx, widths):
    tokens, width = g.shape
    kvb, keep, size, _ = w_value.shape
    return pl.pallas_call(
        first_kernel,
        out_shape=[pltpu.VMEM((tokens, w), BF16) for w in widths],
        in_specs=[HBM] * 5,
        out_specs=[VMEM] * len(widths),
        scratch_shapes=[
            pltpu.VMEM((tokens, width), BF16),
            pltpu.VMEM(w_output.shape, BF16),
            pltpu.VMEM(w_value.shape, BF16),
            pltpu.VMEM((tokens, width), F32),
            pltpu.SMEM(value_idx.shape, jnp.int32),
            pltpu.SMEM(output_idx.shape, jnp.int32),
            pltpu.SemaphoreType.DMA((3,)),
            pltpu.SemaphoreType.DMA((2, kvb)),
        ],
        cost_estimate=cost(4 * tokens * kvb * keep * size * size, 5 << 20),
        name="first",
    )(value_idx, output_idx, g, w_output, w_value)


def second_kernel(vk, ok, o, v, *refs):
    arrived, (out, g, acc) = refs[:-3], refs[-3:]
    at = 0
    for part in arrived:
        wide = part.shape[1]
        g[:, at:at + wide] = part[...]
        acc[:, at:at + wide] = part[...].astype(F32)
        at += wide
    for c in range(o.shape[0]):
        add_back(vk, hidden_grad(ok, g, o, c), v, c, acc)
    write_parts(acc, [out])


def second_call(arrived, w_value, w_output, value_idx, output_idx):
    tokens = arrived[0].shape[0]
    width = sum(part.shape[1] for part in arrived)
    kvb, keep, size, _ = w_value.shape
    return pl.pallas_call(
        second_kernel,
        out_shape=jax.ShapeDtypeStruct((tokens, width), BF16),
        in_specs=[SMEM, SMEM] + [VMEM] * (2 + len(arrived)),
        out_specs=VMEM,
        scratch_shapes=[pltpu.VMEM((tokens, width), BF16), pltpu.VMEM((tokens, width), F32)],
        compiler_params=ROOM,
        cost_estimate=cost(4 * tokens * kvb * keep * size * size, 5 << 20),
        name="second",
    )(value_idx, output_idx, w_output, w_value, *arrived)


def hidden_kernel(vk, x1, x2, v, out, x):
    tokens = x1.shape[0]
    kvb, keep, size, _ = v.shape
    x[:tokens] = x1[...]
    x[tokens:] = x2[...]
    for c in range(kvb):
        total = None
        for both in pairs(keep):
            left = jnp.concatenate([block(x, vk[c, j], size) for j in both], axis=1)
            right = jnp.concatenate([v[c, j] for j in both], axis=0)
            term = lax.dot_general(left, right, NN, preferred_element_type=F32)
            total = term if total is None else total + term
        out[c] = total.astype(BF16).T


def hidden_call(x1, x2, w_value, value_idx):
    tokens, width = x1.shape
    kvb, keep, size, _ = w_value.shape
    return pl.pallas_call(
        hidden_kernel,
        out_shape=pltpu.VMEM((kvb, size, 2 * tokens), BF16),
        in_specs=[SMEM, VMEM, VMEM, VMEM],
        out_specs=VMEM,
        scratch_shapes=[pltpu.VMEM((2 * tokens, width), BF16)],
        compiler_params=ROOM,
        cost_estimate=cost(4 * tokens * kvb * keep * size * size, 3 << 20),
        name="hidden",
    )(value_idx, x1, x2, w_value)


def reverse_bits(value, bits):
    out = 0
    for _ in range(bits):
        out, value = out * 2 + value % 2, value // 2
    return out


def tile_kernel(per, bits, starts, me, ok, h, g, *refs):
    arrived, outs, stack = refs[:-len(starts) - 1], refs[-len(starts) - 1:-1], refs[-1]
    tokens = g.shape[0]
    size = h.shape[1]
    keep = ok.shape[1]
    stack[:tokens] = g[...]
    at = 0
    for part in arrived:
        wide = part.shape[1]
        stack[tokens:, at:at + wide] = part[...]
        at += wide
    flip = me[0] * per
    for out, start in zip(outs, starts):
        for i in range(out.shape[0]):
            position = start + i
            tile = (reverse_bits(position // per, bits) * per + position % per) ^ flip
            c, j = tile // keep, lax.rem(tile, keep)
            term = lax.dot_general(h[c], block(stack, ok[c, j], size), NN, preferred_element_type=F32)
            out[i] = term.astype(out.dtype)


def tile_call(runs, me, output_idx, hidden, g, arrived, ranks):
    kvb, size, stacked = hidden.shape
    keep = output_idx.shape[1]
    total = kvb * keep
    count = sum(n for _, n, _ in runs)
    return pl.pallas_call(
        functools.partial(
            tile_kernel, total // ranks, ranks.bit_length() - 1, [start for start, _, _ in runs]
        ),
        out_shape=[pltpu.VMEM((n, size, size), kind) for _, n, kind in runs],
        in_specs=[SMEM, SMEM] + [VMEM] * (2 + len(arrived)),
        out_specs=[VMEM] * len(runs),
        scratch_shapes=[pltpu.VMEM((stacked, g.shape[1]), BF16)],
        compiler_params=ROOM,
        cost_estimate=cost(2 * stacked * count * size * size, 2 << 20),
        name="tiles",
    )(me, output_idx, hidden, g, *arrived)


def exchange(value, axis, bit):
    count = lax.axis_size(axis)
    return lax.ppermute(value, axis, [(i, i ^ bit) for i in range(count)])


def from_behind(value, axis, steps):
    count = lax.axis_size(axis)
    return lax.ppermute(value, axis, [(i, (i + steps) % count) for i in range(count)])


def per_device(x_first, x_second, grad_first, value_tiles, output_tiles, value_keep, output_keep):
    w_value, w_output = value_tiles[0], output_tiles[0]
    value_idx, output_idx = value_keep[0], output_keep[0]
    g = grad_first[0]
    width = g.shape[1]
    ranks = lax.axis_size("dp")
    me = lax.axis_index("dp").astype(jnp.int32).reshape(1)
    parts = 4
    first = first_call(g, w_value, w_output, value_idx, output_idx, [width // parts] * parts)
    arrived = [from_behind(p, "section", -1) for p in first]
    hidden = hidden_call(x_first[0], x_second[0], w_value, value_idx)
    run = w_value.shape[0] * w_value.shape[1] // 8
    at = {"kd": 0, "kc": 1, "kb": 2, "ka": 3, "sd": 4, "sc": 5, "sb": 6, "sa": 7}
    tiles = functools.partial(
        tile_call, me=me, output_idx=output_idx, hidden=hidden, g=g, arrived=arrived, ranks=ranks
    )
    spec = lambda *names: [(at[n] * run, run, BF16 if n[0] == "s" else F32) for n in names]
    sa, ka = tiles(spec("sa", "ka"))
    got_a = exchange(sa, "dp", 1)
    sc, sb, sd, kc, kb, kd = tiles(spec("sc", "sb", "sd", "kc", "kb", "kd"))
    got_b, got_c, got_d = (exchange(s, "dp", 1) for s in (sb, sc, sd))
    half = run // 2
    out_a = (ka + got_a.astype(F32)).astype(BF16)
    near = [exchange(out_a[i * half:(i + 1) * half], "dp", 2) for i in (0, 1)]
    near_b = exchange((kb + got_b.astype(F32)).astype(BF16), "dp", 2)
    far = []
    for i in (0, 1):
        s = slice(i * half, (i + 1) * half)
        out_c = (kc[s] + got_c[s].astype(F32) + near[i].astype(F32)).astype(BF16)
        if i == 0:
            near[1], out_c = lax.optimization_barrier((near[1], out_c))
        far.append(exchange(out_c, "dp", 4))
    second = second_call(arrived, w_value, w_output, value_idx, output_idx)
    staying = kd + got_d.astype(F32) + near_b.astype(F32)
    staying = staying + jnp.concatenate(far, axis=0).astype(F32)
    bit = 8
    while bit < ranks:
        half = staying.shape[0] // 2
        came = exchange(staying[half:].astype(BF16), "dp", bit)
        staying = staying[:half] + came.astype(F32)
        bit *= 2
    weight_grad = staying * (1.0 / (2.0 * ranks))
    return second[None], weight_grad[None]


def solution(mesh):
    in_specs = (
        P("section", "dp", None),
        P("section", "dp", None),
        P("section", "dp", None),
        P("section", None, None, None, None),
        P("section", None, None, None, None),
        P("section", None, None),
        P("section", None, None),
    )
    out_specs = (P("section", "dp", None), P("section", "dp", None, None))
    return jax.shard_map(
        per_device, mesh=mesh, in_specs=in_specs, out_specs=out_specs, check_vma=False
    )
```

time: 60.7 us -> 50 us (0.82)
  Pallas kernels: 22.8 us -> 12.8 us
  waiting for transfers between devices: 23 us -> 19.1 us
  starting transfers between devices: 10.8 us -> 13.9 us
  local copies, waits for them, and re-layouts: 0.7 us -> 2.13 us
  other arithmetic: 2.38 us -> 1.16 us
    pallas_call x4 -> x5, Pallas kernels: 22.8 us -> 12.8 us  [the longest x1 5.88 us: first_call(): pl.pallas_call(first_kernel, out_shape=[pltpu.VMEM((tokens, w), BF16) for...]
    ppermute x4 -> x9, waiting for transfers between devices: 18.1 us -> 13.3 us  [exchange(): return lax.ppermute(value, axis, [(i, i ^ bit) for i in range(count)])]
    ppermute x4 -> x9, starting transfers between devices: 4.81 us -> 7.88 us  [exchange(): return lax.ppermute(value, axis, [(i, i ^ bit) for i in range(count)])]
    unnamed x10 -> x14, local copies, waits for them, and re-layouts: 0.67 us -> 2.11 us
    convert_element_type x1 -> x4, other arithmetic: 1.36 us -> 0.24 us  [the longest x2 0.11 us: per_device(): out_c = (kc[s] + got_c[s].astype(F32) + near[i].astype(F32)).astype(BF16)]
    ppermute x4, waiting for transfers between devices: 4.95 us -> 5.78 us  [from_behind(): lax.ppermute(value, axis, [(i, (i + steps) % count) for i in range(count)])]
  transfers between devices with their start and end apart: 8 -> 13, of which waited for: 6 -> 7; matrix products, arithmetic and copies ran while one was open for 2% -> 1% of each run, Pallas kernels for 20% -> 12%
where the time goes in v2:
time: 50 us; the launch traced here: 49.8 us
  waiting for transfers between devices  19.1 us (38%)
  starting transfers between devices  13.9 us (28%)
  Pallas kernels  12.8 us (26%)
  local copies, waits for them, and re-layouts  2.13 us (4%)
  other arithmetic  1.16 us (2%)
  between operations  0.75 us (2%)
    ppermute x9, waiting for transfers between devices, exchange(): return lax.ppermute(value, axis, [(i, i ^ bit) for i in range(count)])  13.3 us
    ppermute x9, starting transfers between devices, exchange(): return lax.ppermute(value, axis, [(i, i ^ bit) for i in range(count)])  7.88 us
    ppermute x4, starting transfers between devices, from_behind(): lax.ppermute(value, axis, [(i, (i + steps) % count) for i in range(count)])  6.01 us
    pallas_call x1, Pallas kernels, first_call(): pl.pallas_call(first_kernel, out_shape=[pltpu.VMEM((tokens, w), BF16) for...  5.88 us
    ppermute x4, waiting for transfers between devices, from_behind(): lax.ppermute(value, axis, [(i, (i + steps) % count) for i in range(count)])  5.78 us
    pallas_call x1, Pallas kernels, second_call(): pl.pallas_call(second_kernel, out_shape=jax.ShapeDtypeStruct((tokens, wid...  3.14 us
    pallas_call x2, Pallas kernels, tile_call(): pl.pallas_call(functools.partial(tile_kernel, total // ranks, ranks.bit_l...  2.26 us
    unnamed x14, local copies, waits for them, and re-layouts  2.11 us
  transfers between devices with their start and end apart: 13, of which 7 were waited for; matrix products, arithmetic and copies ran while one was open for 1% of the time, Pallas kernels for 12%

profile of v2, /device:TPU:0, one launch (start us, length us, event | category | flops | bytes accessed | tf_op | source)
XLA Modules:
  0.0 49.8 jit_solution(3110156262799815839)
XLA Ops:
  0.7 5.9 %first.1 = (bf16[64,1024]{1,0:T(8,128)(2,1)}, bf16[64,1024]{1,0:T(8,128)(2,1)S(1)}, bf16[64,1024]{1,0:T(8,128)(2,1)S(1)}, bf16[64,1024]{1,0:T(8,128)(2,1)S(1)}) custom-call(s32[4,16]{1,0:T(4,128)} %bitcast.25, s32[4,16]{1,0:T(4,128)} %bitcast.21, bf16[64,4096]{1,0:T(8,128)(2,1)} %bitcast.16, bf16[4,16,128,128]{3,2,1,0:T(8,128)(2,1)} %bitcast.14, ...), custom_call_target="tpu_custom_call" | custom-call | flops 268435456 | bytes 5242880 | tf_op jit(solution)/shard_map/first/pallas_call | solution.py:87
  6.6 4.0 %collective-permute-start = (bf16[64,1024]{1,0:T(8,128)(2,1)}, bf16[64,1024]{1,0:T(8,128)(2,1)S(1)}, u32[]{:S(2)}, u32[]{:S(2)}) collective-permute-start(bf16[64,1024]{1,0:T(8,128)(2,1)} %get-tuple-element.16), channel_id=1, source_target_pairs={{0,24},{8,0},{16,8},{24,16},{1,25},{9,1},{17,9},{25,17},{2,26},{10... | collective-permute-start | bytes 393224 | tf_op jit(solution)/shard_map/ppermute | solution.py:220
  10.5 0.5 %collective-permute-start.1 = (bf16[64,1024]{1,0:T(8,128)(2,1)S(1)}, bf16[64,1024]{1,0:T(8,128)(2,1)S(1)}, u32[]{:S(2)}, u32[]{:S(2)}) collective-permute-start(bf16[64,1024]{1,0:T(8,128)(2,1)S(1)} %get-tuple-element.17), channel_id=1, source_target_pairs={{0,24},{8,0},{16,8},{24,16},{1,25},{9,1},{17,9},{25,17},{2,26},{10... | collective-permute-start | bytes 393224 | tf_op jit(solution)/shard_map/ppermute | solution.py:220
  11.1 1.4 %collective-permute-start.2 = (bf16[64,1024]{1,0:T(8,128)(2,1)S(1)}, bf16[64,1024]{1,0:T(8,128)(2,1)S(1)}, u32[]{:S(2)}, u32[]{:S(2)}) collective-permute-start(bf16[64,1024]{1,0:T(8,128)(2,1)S(1)} %get-tuple-element.18), channel_id=1, source_target_pairs={{0,24},{8,0},{16,8},{24,16},{1,25},{9,1},{17,9},{25,17},{2,26},{10... | collective-permute-start | bytes 393224 | tf_op jit(solution)/shard_map/ppermute | solution.py:220
  12.6 1.0 %copy-done.3 = bf16[1,64,4096]{2,1,0:T(8,128)(2,1)S(1)} copy-done((bf16[1,64,4096]{2,1,0:T(8,128)(2,1)S(1)}, bf16[1,64,4096]{2,1,0:T(8,128)(2,1)}, u32[]{:S(2)}) %copy-start.3) | copy-done | bytes 524312
  13.6 1.0 %copy-done.4 = bf16[1,64,4096]{2,1,0:T(8,128)(2,1)S(1)} copy-done((bf16[1,64,4096]{2,1,0:T(8,128)(2,1)S(1)}, bf16[1,64,4096]{2,1,0:T(8,128)(2,1)}, u32[]{:S(2)}) %copy-start.4) | copy-done | bytes 524312
  14.7 1.5 %hidden.1.h = bf16[4,128,128]{2,1,0:T(8,128)(2,1)S(1)} custom-call(s32[4,16]{1,0:T(4,128)S(1)} %bitcast.26, bf16[64,4096]{1,0:T(8,128)(2,1)S(1)} %bitcast.19, bf16[64,4096]{1,0:T(8,128)(2,1)S(1)} %bitcast.20, bf16[4,16,128,128]{3,2,1,0:T(8,128)(2,1)S(1)} %bitcast.12), custom_call_target="tpu_custom_call" | custom-call | flops 268435456 | bytes 3145728 | tf_op jit(solution)/shard_map/hidden/pallas_call | solution.py:154
  16.2 1.3 %collective-permute-done.1.refs_1_ = bf16[64,1024]{1,0:T(8,128)(2,1)S(1)} collective-permute-done((bf16[64,1024]{1,0:T(8,128)(2,1)S(1)}, bf16[64,1024]{1,0:T(8,128)(2,1)S(1)}, u32[]{:S(2)}, u32[]{:S(2)}) %collective-permute-start.1) | collective-permute-done | bytes 131104 | tf_op jit(solution)/shard_map/ppermute | solution.py:220
  17.4 2.8 %collective-permute-done.2.refs_2_ = bf16[64,1024]{1,0:T(8,128)(2,1)S(1)} collective-permute-done((bf16[64,1024]{1,0:T(8,128)(2,1)S(1)}, bf16[64,1024]{1,0:T(8,128)(2,1)S(1)}, u32[]{:S(2)}, u32[]{:S(2)}) %collective-permute-start.2) | collective-permute-done | bytes 131104 | tf_op jit(solution)/shard_map/ppermute | solution.py:220
  20.3 1.7 %collective-permute-done.3.refs_3_ = bf16[64,1024]{1,0:T(8,128)(2,1)S(1)} collective-permute-done((bf16[64,1024]{1,0:T(8,128)(2,1)S(1)}, bf16[64,1024]{1,0:T(8,128)(2,1)S(1)}, u32[]{:S(2)}, u32[]{:S(2)}) %collective-permute-start.3) | collective-permute-done | bytes 131104 | tf_op jit(solution)/shard_map/ppermute | solution.py:220
  21.9 1.0 %tiles.3 = (bf16[8,128,128]{2,1,0:T(8,128)(2,1)S(1)}, f32[8,128,128]{2,1,0:T(8,128)S(1)}) custom-call(s32[1]{0:T(128)} %bitcast.6.me, s32[4,16]{1,0:T(4,128)S(1)} %bitcast.22, bf16[4,128,128]{2,1,0:T(8,128)(2,1)S(1)} %hidden.1.h, bf16[64,4096]{1,0:T(8,128)(2,1)S(1)} %bitcast.17, bf16[64,1024]{1,0:T(8,128)(2,1)S(1)} %collective-permute-done.refs_0_, ...), custom_call_target="tpu_custom_call" | custom-call | flops 67108864 | bytes 2097152 | tf_op jit(solution)/shard_map/tiles/pallas_call | solution.py:199
  23.0 1.3 %tiles.2 = (bf16[8,128,128]{2,1,0:T(8,128)(2,1)S(1)}, bf16[8,128,128]{2,1,0:T(8,128)(2,1)S(1)}, bf16[8,128,128]{2,1,0:T(8,128)(2,1)S(1)}, f32[8,128,128]{2,1,0:T...) custom-call(s32[1]{0:T(128)} %bitcast.6.me, s32[4,16]{1,0:T(4,128)S(1)} %bitcast.23, ...), custom_call_target="tpu_custom_call" | custom-call | flops 201326592 | bytes 2097152 | tf_op jit(solution)/shard_map/tiles/pallas_call | solution.py:199
  24.3 0.6 %collective-permute-start.9 = (bf16[8,128,128]{2,1,0:T(8,128)(2,1)S(1)}, bf16[8,128,128]{2,1,0:T(8,128)(2,1)S(1)}, u32[]{:S(2)}, u32[]{:S(2)}) collective-permute-start(bf16[8,128,128]{2,1,0:T(8,128)(2,1)S(1)} %get-tuple-element.27), channel_id=1, source_target_pairs={{0,1},{1,0},{2,3},{3,2},{4,5},{5,4},{6,7},{7,6},{8,9},{9,8},{10,11... | collective-permute-start | bytes 786440 | tf_op jit(solution)/shard_map/ppermute | solution.py:215
  24.9 0.4 collective-permute-start.4
  25.5 1.7 %collective-permute-start.10 = (bf16[4,128,128]{2,1,0:T(8,128)(2,1)S(1)}, bf16[4,128,128]{2,1,0:T(8,128)(2,1)S(1)}, u32[]{:S(2)}, u32[]{:S(2)}) collective-permute-start(bf16[4,128,128]{2,1,0:T(8,128)(2,1)S(1)} %get-tuple-element.30), channel_id=1, source_target_pairs={{0,2},{1,3},{2,0},{3,1},{4,6},{5,7},{6,4},{7,5},{8,10},{9,11},{10,... | collective-permute-start | bytes 393224 | tf_op jit(solution)/shard_map/ppermute | solution.py:215
  27.1 0.4 collective-permute-start.8
  27.6 1.7 %collective-permute-start.6 = (bf16[8,128,128]{2,1,0:T(8,128)(2,1)S(1)}, bf16[8,128,128]{2,1,0:T(8,128)(2,1)S(1)}, u32[]{:S(2)}, u32[]{:S(2)}) collective-permute-start(bf16[8,128,128]{2,1,0:T(8,128)(2,1)S(1)} %add_convert_fusion.1), channel_id=1, source_target_pairs={{0,2},{1,3},{2,0},{3,1},{4,6},{5,7},{6,4},{7,5},{8,10},{9,11},{10,... | collective-permute-start | bytes 786440 | tf_op jit(solution)/shard_map/ppermute | solution.py:215
  29.3 2.6 %collective-permute-done.10 = bf16[4,128,128]{2,1,0:T(8,128)(2,1)S(1)} collective-permute-done((bf16[4,128,128]{2,1,0:T(8,128)(2,1)S(1)}, bf16[4,128,128]{2,1,0:T(8,128)(2,1)S(1)}, u32[]{:S(2)}, u32[]{:S(2)}) %collective-permute-start.10) | collective-permute-done | bytes 131104 | tf_op jit(solution)/shard_map/ppermute | solution.py:215
  32.0 2.7 %collective-permute-done.8 = bf16[4,128,128]{2,1,0:T(8,128)(2,1)S(1)} collective-permute-done((bf16[4,128,128]{2,1,0:T(8,128)(2,1)S(1)}, bf16[4,128,128]{2,1,0:T(8,128)(2,1)S(1)}, u32[]{:S(2)}, u32[]{:S(2)}) %collective-permute-start.8) | collective-permute-done | bytes 131104 | tf_op jit(solution)/shard_map/ppermute | solution.py:215
  34.8 2.7 %collective-permute-start.12 = (bf16[4,128,128]{2,1,0:T(8,128)(2,1)S(1)}, bf16[4,128,128]{2,1,0:T(8,128)(2,1)S(1)}, u32[]{:S(2)}, u32[]{:S(2)}) collective-permute-start(bf16[4,128,128]{2,1,0:T(8,128)(2,1)S(1)} %add_convert_fusion.2), channel_id=1, source_target_pairs={{0,4},{1,5},{2,6},{3,7},{4,0},{5,1},{6,2},{7,3},{8,12},{9,13},{10,... | collective-permute-start | bytes 393224 | tf_op jit(solution)/shard_map/ppermute | solution.py:215
  37.8 3.1 %second.1 = bf16[64,4096]{1,0:T(8,128)(2,1)} custom-call(s32[4,16]{1,0:T(4,128)S(1)} %bitcast.27, s32[4,16]{1,0:T(4,128)S(1)} %bitcast.24, bf16[4,16,128,128]{3,2,1,0:T(8,128)(2,1)S(1)} %bitcast.15, bf16[4,16,128,128]{3,2,1,0:T(8,128)(2,1)S(1)} %bitcast.13, bf16[64,1024]{1,0:T(8,128)(2,1)S(1)} %collective-permute-done.refs_0_, ...), custom_call_target="tpu_custom_call" | custom-call | flops 268435456 | bytes 5242880 | tf_op jit(solution)/shard_map/second/pallas_call | solution.py:124
  40.9 6.6 %collective-permute-done.12 = bf16[4,128,128]{2,1,0:T(8,128)(2,1)S(1)} collective-permute-done((bf16[4,128,128]{2,1,0:T(8,128)(2,1)S(1)}, bf16[4,128,128]{2,1,0:T(8,128)(2,1)S(1)}, u32[]{:S(2)}, u32[]{:S(2)}) %collective-permute-start.12) | collective-permute-done | bytes 131104 | tf_op jit(solution)/shard_map/ppermute | solution.py:215
  47.5 1.4 %collective-permute-done.11 = bf16[4,128,128]{2,1,0:T(8,128)(2,1)S(1)} collective-permute-done((bf16[4,128,128]{2,1,0:T(8,128)(2,1)S(1)}, bf16[4,128,128]{2,1,0:T(8,128)(2,1)S(1)}, u32[]{:S(2)}, u32[]{:S(2)}) %collective-permute-start.11) | collective-permute-done | bytes 131104 | tf_op jit(solution)/shard_map/ppermute | solution.py:215
  48.9 0.9 %multiply_bitcast_fusion = f32[1,8,128,128]{3,2,1,0:T(8,128)} fusion(bf16[8,128,128]{2,1,0:T(8,128)(2,1)S(1)} %collective-permute-done.6, f32[8,128,128]{2,1,0:T(8,128)S(1)} %get-tuple-element.20, bf16[8,128,128]{2,1,0:T(8,128)(2,1)S(1)} %collective-permute-done.4, bf16[4,128,128]{2,1,0:T(8,128)(2,1)S(1)} %collective-permute-done.12, ...), kind=kLoop, calls=%fused_computation | loop fusion | flops 1048576 | bytes 1835008 | tf_op jit(solution)/shard_map/broadcast_in_dim | solution.py:265
  (27 shorter events, 0.8 us)
Async XLA Ops:
  0.6 11.9 %copy-start = (bf16[1,4,16,128,128]{4,3,2,1,0:T(8,128)(2,1)S(1)}, bf16[1,4,16,128,128]{4,3,2,1,0:T(8,128)(2,1)}, u32[]{:S(2)}) copy-start(bf16[1,4,16,128,128]{4,3,2,1,0:T(8,128)(2,1)} %param.10) | copy-start | bytes 6291460
  0.6 11.9 %copy-start.6 = (s32[1,4,16]{2,1,0:T(4,128)S(1)}, s32[1,4,16]{2,1,0:T(4,128)}, u32[]{:S(2)}) copy-start(s32[1,4,16]{2,1,0:T(4,128)} %param.12) | copy-start | bytes 772
  0.7 21.3 %copy-start.5 = (s32[1,4,16]{2,1,0:T(4,128)S(1)}, s32[1,4,16]{2,1,0:T(4,128)}, u32[]{:S(2)}) copy-start(s32[1,4,16]{2,1,0:T(4,128)} %param.13) | copy-start | bytes 772
  6.6 15.4 %copy-start.2 = (bf16[1,64,4096]{2,1,0:T(8,128)(2,1)S(1)}, bf16[1,64,4096]{2,1,0:T(8,128)(2,1)}, u32[]{:S(2)}) copy-start(bf16[1,64,4096]{2,1,0:T(8,128)(2,1)} %param.9) | copy-start | bytes 1572868
  6.6 9.6 %collective-permute-start = (bf16[64,1024]{1,0:T(8,128)(2,1)}, bf16[64,1024]{1,0:T(8,128)(2,1)S(1)}, u32[]{:S(2)}, u32[]{:S(2)}) collective-permute-start(bf16[64,1024]{1,0:T(8,128)(2,1)} %get-tuple-element.16), channel_id=1, source_target_pairs={{0,24},{8,0},{16,8},{24,16},{1,25},{9,1},{17,9},{25,17},{2,26},{10... | collective-permute-start | bytes 393224 | tf_op jit(solution)/shard_map/ppermute | solution.py:220
  10.5 6.9 %collective-permute-start.1 = (bf16[64,1024]{1,0:T(8,128)(2,1)S(1)}, bf16[64,1024]{1,0:T(8,128)(2,1)S(1)}, u32[]{:S(2)}, u32[]{:S(2)}) collective-permute-start(bf16[64,1024]{1,0:T(8,128)(2,1)S(1)} %get-tuple-element.17), channel_id=1, source_target_pairs={{0,24},{8,0},{16,8},{24,16},{1,25},{9,1},{17,9},{25,17},{2,26},{10... | collective-permute-start | bytes 393224 | tf_op jit(solution)/shard_map/ppermute | solution.py:220
  11.1 9.2 %collective-permute-start.2 = (bf16[64,1024]{1,0:T(8,128)(2,1)S(1)}, bf16[64,1024]{1,0:T(8,128)(2,1)S(1)}, u32[]{:S(2)}, u32[]{:S(2)}) collective-permute-start(bf16[64,1024]{1,0:T(8,128)(2,1)S(1)} %get-tuple-element.18), channel_id=1, source_target_pairs={{0,24},{8,0},{16,8},{24,16},{1,25},{9,1},{17,9},{25,17},{2,26},{10... | collective-permute-start | bytes 393224 | tf_op jit(solution)/shard_map/ppermute | solution.py:220
  12.5 9.4 %collective-permute-start.3 = (bf16[64,1024]{1,0:T(8,128)(2,1)S(1)}, bf16[64,1024]{1,0:T(8,128)(2,1)S(1)}, u32[]{:S(2)}, u32[]{:S(2)}) collective-permute-start(bf16[64,1024]{1,0:T(8,128)(2,1)S(1)} %get-tuple-element.19), channel_id=1, source_target_pairs={{0,24},{8,0},{16,8},{24,16},{1,25},{9,1},{17,9},{25,17},{2,26},{10... | collective-permute-start | bytes 393224 | tf_op jit(solution)/shard_map/ppermute | solution.py:220
  12.6 1.0 %copy-start.3 = (bf16[1,64,4096]{2,1,0:T(8,128)(2,1)S(1)}, bf16[1,64,4096]{2,1,0:T(8,128)(2,1)}, u32[]{:S(2)}) copy-start(bf16[1,64,4096]{2,1,0:T(8,128)(2,1)} %param.7) | copy-start | bytes 1572868
  13.6 1.0 %copy-start.4 = (bf16[1,64,4096]{2,1,0:T(8,128)(2,1)S(1)}, bf16[1,64,4096]{2,1,0:T(8,128)(2,1)}, u32[]{:S(2)}) copy-start(bf16[1,64,4096]{2,1,0:T(8,128)(2,1)} %param.8) | copy-start | bytes 1572868
  22.9 2.5 %collective-permute-start.7 = (bf16[8,128,128]{2,1,0:T(8,128)(2,1)S(1)}, bf16[8,128,128]{2,1,0:T(8,128)(2,1)S(1)}, u32[]{:S(2)}, u32[]{:S(2)}) collective-permute-start(bf16[8,128,128]{2,1,0:T(8,128)(2,1)S(1)} %get-tuple-element.25), channel_id=1, source_target_pairs={{0,1},{1,0},{2,3},{3,2},{4,5},{5,4},{6,7},{7,6},{8,9},{9,8},{10,11... | collective-permute-start | bytes 786440 | tf_op jit(solution)/shard_map/ppermute | solution.py:215
  24.3 13.5 %copy-start.1 = (bf16[1,4,16,128,128]{4,3,2,1,0:T(8,128)(2,1)S(1)}, bf16[1,4,16,128,128]{4,3,2,1,0:T(8,128)(2,1)}, u32[]{:S(2)}) copy-start(bf16[1,4,16,128,128]{4,3,2,1,0:T(8,128)(2,1)} %param.11) | copy-start | bytes 6291460
  24.3 5.0 %collective-permute-start.9 = (bf16[8,128,128]{2,1,0:T(8,128)(2,1)S(1)}, bf16[8,128,128]{2,1,0:T(8,128)(2,1)S(1)}, u32[]{:S(2)}, u32[]{:S(2)}) collective-permute-start(bf16[8,128,128]{2,1,0:T(8,128)(2,1)S(1)} %get-tuple-element.27), channel_id=1, source_target_pairs={{0,1},{1,0},{2,3},{3,2},{4,5},{5,4},{6,7},{7,6},{8,9},{9,8},{10,11... | collective-permute-start | bytes 786440 | tf_op jit(solution)/shard_map/ppermute | solution.py:215
  24.9 2.7 %collective-permute-start.5 = (bf16[8,128,128]{2,1,0:T(8,128)(2,1)S(1)}, bf16[8,128,128]{2,1,0:T(8,128)(2,1)S(1)}, u32[]{:S(2)}, u32[]{:S(2)}) collective-permute-start(bf16[8,128,128]{2,1,0:T(8,128)(2,1)S(1)} %get-tuple-element.23), channel_id=1, source_target_pairs={{0,1},{1,0},{2,3},{3,2},{4,5},{5,4},{6,7},{7,6},{8,9},{9,8},{10,11... | collective-permute-start | bytes 786440 | tf_op jit(solution)/shard_map/ppermute | solution.py:215
  24.9 16.0 %collective-permute-start.4 = (bf16[8,128,128]{2,1,0:T(8,128)(2,1)S(1)}, bf16[8,128,128]{2,1,0:T(8,128)(2,1)S(1)}, u32[]{:S(2)}, u32[]{:S(2)}) collective-permute-start(bf16[8,128,128]{2,1,0:T(8,128)(2,1)S(1)} %get-tuple-element.21), channel_id=1, source_target_pairs={{0,1},{1,0},{2,3},{3,2},{4,5},{5,4},{6,7},{7,6},{8,9},{9,8},{10,11... | collective-permute-start | bytes 786440 | tf_op jit(solution)/shard_map/ppermute | solution.py:215
  25.5 6.4 %collective-permute-start.10 = (bf16[4,128,128]{2,1,0:T(8,128)(2,1)S(1)}, bf16[4,128,128]{2,1,0:T(8,128)(2,1)S(1)}, u32[]{:S(2)}, u32[]{:S(2)}) collective-permute-start(bf16[4,128,128]{2,1,0:T(8,128)(2,1)S(1)} %get-tuple-element.30), channel_id=1, source_target_pairs={{0,2},{1,3},{2,0},{3,1},{4,6},{5,7},{6,4},{7,5},{8,10},{9,11},{10,... | collective-permute-start | bytes 393224 | tf_op jit(solution)/shard_map/ppermute | solution.py:215
  27.1 7.6 %collective-permute-start.8 = (bf16[4,128,128]{2,1,0:T(8,128)(2,1)S(1)}, bf16[4,128,128]{2,1,0:T(8,128)(2,1)S(1)}, u32[]{:S(2)}, u32[]{:S(2)}) collective-permute-start(bf16[4,128,128]{2,1,0:T(8,128)(2,1)S(1)} %get-tuple-element.31), channel_id=1, source_target_pairs={{0,2},{1,3},{2,0},{3,1},{4,6},{5,7},{6,4},{7,5},{8,10},{9,11},{10,... | collective-permute-start | bytes 393224 | tf_op jit(solution)/shard_map/ppermute | solution.py:215
  27.6 21.2 %collective-permute-start.6 = (bf16[8,128,128]{2,1,0:T(8,128)(2,1)S(1)}, bf16[8,128,128]{2,1,0:T(8,128)(2,1)S(1)}, u32[]{:S(2)}, u32[]{:S(2)}) collective-permute-start(bf16[8,128,128]{2,1,0:T(8,128)(2,1)S(1)} %add_convert_fusion.1), channel_id=1, source_target_pairs={{0,2},{1,3},{2,0},{3,1},{4,6},{5,7},{6,4},{7,5},{8,10},{9,11},{10,... | collective-permute-start | bytes 786440 | tf_op jit(solution)/shard_map/ppermute | solution.py:215
  34.8 12.7 %collective-permute-start.12 = (bf16[4,128,128]{2,1,0:T(8,128)(2,1)S(1)}, bf16[4,128,128]{2,1,0:T(8,128)(2,1)S(1)}, u32[]{:S(2)}, u32[]{:S(2)}) collective-permute-start(bf16[4,128,128]{2,1,0:T(8,128)(2,1)S(1)} %add_convert_fusion.2), channel_id=1, source_target_pairs={{0,4},{1,5},{2,6},{3,7},{4,0},{5,1},{6,2},{7,3},{8,12},{9,13},{10,... | collective-permute-start | bytes 393224 | tf_op jit(solution)/shard_map/ppermute | solution.py:215
  37.4 11.4 %collective-permute-start.11 = (bf16[4,128,128]{2,1,0:T(8,128)(2,1)S(1)}, bf16[4,128,128]{2,1,0:T(8,128)(2,1)S(1)}, u32[]{:S(2)}, u32[]{:S(2)}) collective-permute-start(bf16[4,128,128]{2,1,0:T(8,128)(2,1)S(1)} %add_convert_fusion.3), channel_id=1, source_target_pairs={{0,4},{1,5},{2,6},{3,7},{4,0},{5,1},{6,2},{7,3},{8,12},{9,13},{10,... | collective-permute-start | bytes 393224 | tf_op jit(solution)/shard_map/ppermute | solution.py:215

commit v3 on v2

--- a/solution.py
+++ b/solution.py
@@ -6,6 +6,7 @@
 from jax.experimental import pallas as pl
 from jax.experimental.pallas import tpu as pltpu
 from jax.sharding import PartitionSpec as P
+
 
 F32 = jnp.float32
 BF16 = jnp.bfloat16
@@ -15,6 +16,7 @@
 SMEM = pl.BlockSpec(memory_space=pltpu.SMEM)
 HBM = pl.BlockSpec(memory_space=pl.ANY)
 ROOM = pltpu.CompilerParams(vmem_limit_bytes=16 << 20)
+FULL = pltpu.CompilerParams(vmem_limit_bytes=60 * 1024 * 1024)
 
 
 def cost(flops, nbytes):
@@ -104,41 +106,73 @@
     )(value_idx, output_idx, g, w_output, w_value)
 
 
-def second_kernel(vk, ok, o, v, *refs):
-    arrived, (out, g, acc) = refs[:-3], refs[-3:]
+def fetch(sources, targets, sem):
+    copies = [pltpu.make_async_copy(a, b, sem.at[i]) for i, (a, b) in enumerate(zip(sources, targets))]
+    for copy in copies:
+        copy.start()
+    return copies
+
+
+def second_kernel(count, vk_hbm, ok_hbm, o_hbm, v_hbm, *refs):
+    parts, (out, o, v, g, acc, vk, ok, sem) = refs[:count], refs[count:]
+    kvb = o.shape[0]
+    both = [r.at[c] for r in (o_hbm, v_hbm) for c in range(kvb)]
+    into = [r.at[c] for r in (o, v) for c in range(kvb)]
+    copies = fetch([ok_hbm, vk_hbm] + both, [ok, vk] + into, sem)
     at = 0
-    for part in arrived:
+    for part in parts:
         wide = part.shape[1]
         g[:, at:at + wide] = part[...]
         acc[:, at:at + wide] = part[...].astype(F32)
         at += wide
-    for c in range(o.shape[0]):
-        add_back(vk, hidden_grad(ok, g, o, c), v, c, acc)
-    write_parts(acc, [out])
-
-
-def second_call(arrived, w_value, w_output, value_idx, output_idx):
-    tokens = arrived[0].shape[0]
-    width = sum(part.shape[1] for part in arrived)
+    copies[0].wait()
+    hidden = []
+    for c in range(kvb):
+        copies[2 + c].wait()
+        hidden.append(hidden_grad(ok, g, o, c))
+    copies[1].wait()
+    for c in range(kvb):
+        copies[2 + kvb + c].wait()
+        add_back(vk, hidden[c], v, c, acc)
+    out[...] = acc[...].astype(BF16)
+
+
+def second_call(parts, w_value, w_output, value_idx, output_idx):
+    tokens = parts[0].shape[0]
+    width = sum(part.shape[1] for part in parts)
     kvb, keep, size, _ = w_value.shape
     return pl.pallas_call(
-        second_kernel,
+        functools.partial(second_kernel, len(parts)),
         out_shape=jax.ShapeDtypeStruct((tokens, width), BF16),
-        in_specs=[SMEM, SMEM] + [VMEM] * (2 + len(arrived)),
+        in_specs=[HBM] * 4 + [VMEM] * len(parts),
         out_specs=VMEM,
-        scratch_shapes=[pltpu.VMEM((tokens, width), BF16), pltpu.VMEM((tokens, width), F32)],
-        compiler_params=ROOM,
+        scratch_shapes=[
+            pltpu.VMEM(w_output.shape, BF16),
+            pltpu.VMEM(w_value.shape, BF16),
+            pltpu.VMEM((tokens, width), BF16),
+            pltpu.VMEM((tokens, width), F32),
+            pltpu.SMEM(value_idx.shape, jnp.int32),
+            pltpu.SMEM(output_idx.shape, jnp.int32),
+            pltpu.SemaphoreType.DMA((2 + 2 * kvb,)),
+        ],
+        compiler_params=FULL,
         cost_estimate=cost(4 * tokens * kvb * keep * size * size, 5 << 20),
         name="second",
-    )(value_idx, output_idx, w_output, w_value, *arrived)
-
-
-def hidden_kernel(vk, x1, x2, v, out, x):
+    )(value_idx, output_idx, w_output, w_value, *parts)
+
+
+def hidden_kernel(vk, x1, x2, v_hbm, out, x, v, sem):
     tokens = x1.shape[0]
     kvb, keep, size, _ = v.shape
-    x[:tokens] = x1[...]
-    x[tokens:] = x2[...]
-    for c in range(kvb):
+    copies = fetch(
+        [x1, x2] + [v_hbm.at[c] for c in range(kvb)],
+        [x.at[pl.ds(0, tokens)], x.at[pl.ds(tokens, tokens)]] + [v.at[c] for c in range(kvb)],
+        sem,
+    )
+    copies[0].wait()
+    copies[1].wait()
+    for c in range(kvb):
+        copies[2 + c].wait()
         total = None
         for both in pairs(keep):
             left = jnp.concatenate([block(x, vk[c, j], size) for j in both], axis=1)
@@ -154,10 +188,14 @@
     return pl.pallas_call(
         hidden_kernel,
         out_shape=pltpu.VMEM((kvb, size, 2 * tokens), BF16),
-        in_specs=[SMEM, VMEM, VMEM, VMEM],
+        in_specs=[SMEM, HBM, HBM, HBM],
         out_specs=VMEM,
-        scratch_shapes=[pltpu.VMEM((2 * tokens, width), BF16)],
-        compiler_params=ROOM,
+        scratch_shapes=[
+            pltpu.VMEM((2 * tokens, width), BF16),
+            pltpu.VMEM(w_value.shape, BF16),
+            pltpu.SemaphoreType.DMA((2 + kvb,)),
+        ],
+        compiler_params=FULL,
         cost_estimate=cost(4 * tokens * kvb * keep * size * size, 3 << 20),
         name="hidden",
     )(value_idx, x1, x2, w_value)
@@ -241,19 +279,21 @@
     got_a = exchange(sa, "dp", 1)
     sc, sb, sd, kc, kb, kd = tiles(spec("sc", "sb", "sd", "kc", "kb", "kd"))
     got_b, got_c, got_d = (exchange(s, "dp", 1) for s in (sb, sc, sd))
-    half = run // 2
+    cuts = [slice(0, run // 4), slice(run // 4, run)]
     out_a = (ka + got_a.astype(F32)).astype(BF16)
-    near = [exchange(out_a[i * half:(i + 1) * half], "dp", 2) for i in (0, 1)]
+    near = []
+    for cut in cuts:
+        near.append(exchange(out_a[cut], "dp", 2))
     near_b = exchange((kb + got_b.astype(F32)).astype(BF16), "dp", 2)
     far = []
-    for i in (0, 1):
-        s = slice(i * half, (i + 1) * half)
-        out_c = (kc[s] + got_c[s].astype(F32) + near[i].astype(F32)).astype(BF16)
+    for i, cut in enumerate(cuts):
+        out_c = (kc[cut] + got_c[cut].astype(F32) + near[i].astype(F32)).astype(BF16)
         if i == 0:
-            near[1], out_c = lax.optimization_barrier((near[1], out_c))
+            near[1], _ = lax.optimization_barrier((near[1], out_c))
         far.append(exchange(out_c, "dp", 4))
     second = second_call(arrived, w_value, w_output, value_idx, output_idx)
     staying = kd + got_d.astype(F32) + near_b.astype(F32)
+    staying, far = lax.optimization_barrier((staying, far))
     staying = staying + jnp.concatenate(far, axis=0).astype(F32)
     bit = 8
     while bit < ranks:
@@ -276,6 +316,7 @@
         P("section", None, None),
     )
     out_specs = (P("section", "dp", None), P("section", "dp", None, None))
+
     return jax.shard_map(
         per_device, mesh=mesh, in_specs=in_specs, out_specs=out_specs, check_vma=False
     )

time: 50 us -> 56.9 us (1.14)
  Pallas kernels: 12.8 us -> 18.1 us
  other arithmetic: 1.16 us -> 4.81 us
  local copies, waits for them, and re-layouts: 2.13 us -> 0.05 us
  waiting for transfers between devices: 19.1 us -> 17.5 us
  starting transfers between devices: 13.9 us -> 15.4 us
    pallas_call x1, Pallas kernels: 3.14 us -> 5.99 us  [second_call(): pl.pallas_call(functools.partial(second_kernel, len(parts)), out_shape=ja...]
    unnamed x14 -> x12, local copies, waits for them, and re-layouts: 2.11 us -> 0.03 us
    pallas_call x1, Pallas kernels: 1.48 us -> 3.53 us  [hidden_call(): pl.pallas_call(hidden_kernel, out_shape=pltpu.VMEM((kvb, size, 2 * tokens...]
    convert_element_type x2, other arithmetic: 0.11 us -> 1.86 us  [per_device(): (kc[cut] + got_c[cut].astype(F32) + near[i].astype(F32)).astype(BF16)]
    ppermute x9, starting transfers between devices: 7.88 us -> 9.42 us  [exchange(): return lax.ppermute(value, axis, [(i, i ^ bit) for i in range(count)])]
    ppermute x9, waiting for transfers between devices: 13.3 us -> 11.9 us  [exchange(): return lax.ppermute(value, axis, [(i, i ^ bit) for i in range(count)])]
    pallas_call x2, Pallas kernels: 2.26 us -> 3.42 us  [tile_call(): pl.pallas_call(functools.partial(tile_kernel, total // ranks, ranks.bit_l...]
    convert_element_type x1, other arithmetic: 0.06 us -> 1.01 us  [per_device(): out_a = (ka + got_a.astype(F32)).astype(BF16)]
  transfers between devices with their start and end apart: 13 -> 13, of which waited for: 7 -> 6; matrix products, arithmetic and copies ran while one was open for 1% -> 7% of each run, Pallas kernels for 12% -> 20%
where the time goes in v3:
time: 56.9 us; the launch traced here: 56.6 us
  Pallas kernels  18.1 us (32%)
  waiting for transfers between devices  17.5 us (31%)
  starting transfers between devices  15.4 us (27%)
  other arithmetic  4.81 us (8%)
  between operations  0.75 us (1%)
    ppermute x9, waiting for transfers between devices, exchange(): return lax.ppermute(value, axis, [(i, i ^ bit) for i in range(count)])  11.9 us
    ppermute x9, starting transfers between devices, exchange(): return lax.ppermute(value, axis, [(i, i ^ bit) for i in range(count)])  9.42 us
    ppermute x4, starting transfers between devices, from_behind(): lax.ppermute(value, axis, [(i, (i + steps) % count) for i in range(count)])  6 us
    pallas_call x1, Pallas kernels, second_call(): pl.pallas_call(functools.partial(second_kernel, len(parts)), out_shape=ja...  5.99 us
    ppermute x4, waiting for transfers between devices, from_behind(): lax.ppermute(value, axis, [(i, (i + steps) % count) for i in range(count)])  5.59 us
    pallas_call x1, Pallas kernels, first_call(): pl.pallas_call(first_kernel, out_shape=[pltpu.VMEM((tokens, w), BF16) for...  5.13 us
    pallas_call x1, Pallas kernels, hidden_call(): pl.pallas_call(hidden_kernel, out_shape=pltpu.VMEM((kvb, size, 2 * tokens...  3.53 us
    pallas_call x2, Pallas kernels, tile_call(): pl.pallas_call(functools.partial(tile_kernel, total // ranks, ranks.bit_l...  3.42 us
  transfers between devices with their start and end apart: 13, of which 6 were waited for; matrix products, arithmetic and copies ran while one was open for 7% of the time, Pallas kernels for 20%

profile of v3, /device:TPU:0, one launch (start us, length us, event | category | flops | bytes accessed | tf_op | source)
XLA Modules:
  0.0 56.6 jit_solution(17018677437005802431)
XLA Ops:
  0.6 5.1 %first.1 = (bf16[64,1024]{1,0:T(8,128)(2,1)S(1)}, bf16[64,1024]{1,0:T(8,128)(2,1)S(1)}, bf16[64,1024]{1,0:T(8,128)(2,1)S(1)}, bf16[64,1024]{1,0:T(8,128)(2,1)S(1)}) custom-call(s32[4,16]{1,0:T(4,128)} %bitcast.26, s32[4,16]{1,0:T(4,128)} %bitcast.14, bf16[64,4096]{1,0:T(8,128)(2,1)} %bitcast.11, bf16[4,16,128,128]{3,2,1,0:T(8,128)(2,1)} %bitcast.21, ...), custom_call_target="tpu_custom_call" | custom-call | flops 268435456 | bytes 5242880 | tf_op jit(solution)/shard_map/first/pallas_call | solution.py:89
  5.8 4.0 %collective-permute-start = (bf16[64,1024]{1,0:T(8,128)(2,1)S(1)}, bf16[64,1024]{1,0:T(8,128)(2,1)S(1)}, u32[]{:S(2)}, u32[]{:S(2)}) collective-permute-start(bf16[64,1024]{1,0:T(8,128)(2,1)S(1)} %get-tuple-element.18), channel_id=1, source_target_pairs={{0,24},{8,0},{16,8},{24,16},{1,25},{9,1},{17,9},{25,17},{2,26},{10... | collective-permute-start | bytes 393224 | tf_op jit(solution)/shard_map/ppermute | solution.py:258
  9.8 0.5 collective-permute-start.1
  10.3 1.4 %collective-permute-start.2 = (bf16[64,1024]{1,0:T(8,128)(2,1)S(1)}, bf16[64,1024]{1,0:T(8,128)(2,1)S(1)}, u32[]{:S(2)}, u32[]{:S(2)}) collective-permute-start(bf16[64,1024]{1,0:T(8,128)(2,1)S(1)} %get-tuple-element.20), channel_id=1, source_target_pairs={{0,24},{8,0},{16,8},{24,16},{1,25},{9,1},{17,9},{25,17},{2,26},{10... | collective-permute-start | bytes 393224 | tf_op jit(solution)/shard_map/ppermute | solution.py:258
  11.8 3.5 %hidden.1.h = bf16[4,128,128]{2,1,0:T(8,128)(2,1)S(1)} custom-call(s32[4,16]{1,0:T(4,128)} %bitcast.27, bf16[64,4096]{1,0:T(8,128)(2,1)} %bitcast.24, bf16[64,4096]{1,0:T(8,128)(2,1)} %bitcast.25, bf16[4,16,128,128]{3,2,1,0:T(8,128)(2,1)} %bitcast.19), custom_call_target="tpu_custom_call" | custom-call | flops 268435456 | bytes 3145728 | tf_op jit(solution)/shard_map/hidden/pallas_call | solution.py:188
  15.4 1.1 %collective-permute-done.1.refs_1_ = bf16[64,1024]{1,0:T(8,128)(2,1)S(1)} collective-permute-done((bf16[64,1024]{1,0:T(8,128)(2,1)S(1)}, bf16[64,1024]{1,0:T(8,128)(2,1)S(1)}, u32[]{:S(2)}, u32[]{:S(2)}) %collective-permute-start.1) | collective-permute-done | bytes 131104 | tf_op jit(solution)/shard_map/ppermute | solution.py:258
  16.5 2.8 %collective-permute-done.2.refs_2_ = bf16[64,1024]{1,0:T(8,128)(2,1)S(1)} collective-permute-done((bf16[64,1024]{1,0:T(8,128)(2,1)S(1)}, bf16[64,1024]{1,0:T(8,128)(2,1)S(1)}, u32[]{:S(2)}, u32[]{:S(2)}) %collective-permute-start.2) | collective-permute-done | bytes 131104 | tf_op jit(solution)/shard_map/ppermute | solution.py:258
  19.3 1.7 %collective-permute-done.3.refs_3_ = bf16[64,1024]{1,0:T(8,128)(2,1)S(1)} collective-permute-done((bf16[64,1024]{1,0:T(8,128)(2,1)S(1)}, bf16[64,1024]{1,0:T(8,128)(2,1)S(1)}, u32[]{:S(2)}, u32[]{:S(2)}) %collective-permute-start.3) | collective-permute-done | bytes 131104 | tf_op jit(solution)/shard_map/ppermute | solution.py:258
  21.0 1.6 %tiles.3 = (bf16[8,128,128]{2,1,0:T(8,128)(2,1)}, f32[8,128,128]{2,1,0:T(8,128)S(1)}) custom-call(s32[1]{0:T(128)} %bitcast.6.me, s32[4,16]{1,0:T(4,128)S(1)} %bitcast.16, bf16[4,128,128]{2,1,0:T(8,128)(2,1)S(1)} %hidden.1.h, bf16[64,4096]{1,0:T(8,128)(2,1)S(1)} %bitcast.12, bf16[64,1024]{1,0:T(8,128)(2,1)S(1)} %collective-permute-done.refs_0_, ...), custom_call_target="tpu_custom_call" | custom-call | flops 67108864 | bytes 2097152 | tf_op jit(solution)/shard_map/tiles/pallas_call | solution.py:237
  22.5 1.9 %tiles.2 = (bf16[8,128,128]{2,1,0:T(8,128)(2,1)S(1)}, bf16[8,128,128]{2,1,0:T(8,128)(2,1)}, bf16[8,128,128]{2,1,0:T(8,128)(2,1)S(1)}, f32[8,128,128]{2,1,0:T(8,1...) custom-call(s32[1]{0:T(128)} %bitcast.6.me, s32[4,16]{1,0:T(4,128)S(1)} %bitcast.17, ...), custom_call_target="tpu_custom_call" | custom-call | flops 201326592 | bytes 2097152 | tf_op jit(solution)/shard_map/tiles/pallas_call | solution.py:237
  24.4 0.5 collective-permute-start.7
  25.4 6.0 %second.1 = bf16[64,4096]{1,0:T(8,128)(2,1)} custom-call(s32[4,16]{1,0:T(4,128)} %bitcast.28, s32[4,16]{1,0:T(4,128)} %bitcast.15, bf16[4,16,128,128]{3,2,1,0:T(8,128)(2,1)} %bitcast.22, bf16[4,16,128,128]{3,2,1,0:T(8,128)(2,1)} %bitcast.20, bf16[64,1024]{1,0:T(8,128)(2,1)} %copy-done.1, bf16[64,1024]{1,0:T(8,128)(2,1)} %copy-done.2, ...), custom_call_target="tpu_custom_call" | custom-call | flops 268435456 | bytes 5242880 | tf_op jit(solution)/shard_map/second/pallas_call | solution.py:144
  31.4 1.0 %add_convert_fusion = bf16[8,128,128]{2,1,0:T(8,128)(2,1)S(1)} fusion(f32[8,128,128]{2,1,0:T(8,128)S(1)} %get-tuple-element.28, bf16[8,128,128]{2,1,0:T(8,128)(2,1)} %collective-permute-done.8), kind=kLoop, calls=%fused_computation.1 | loop fusion | flops 393216 | bytes 1048576 | tf_op jit(solution)/shard_map/convert_element_type | solution.py:283
  32.5 1.7 %collective-permute-start.9 = (bf16[2,128,128]{2,1,0:T(8,128)(2,1)S(1)}, bf16[2,128,128]{2,1,0:T(8,128)(2,1)S(1)}, u32[]{:S(2)}, u32[]{:S(2)}) collective-permute-start(bf16[2,128,128]{2,1,0:T(8,128)(2,1)S(1)} %slice.25), channel_id=1, source_target_pairs={{0,2},{1,3},{2,0},{3,1},{4,6},{5,7},{6,4},{7,5},{8,10},{9,11},{10,... | collective-permute-start | bytes 196616 | tf_op jit(solution)/shard_map/ppermute | solution.py:253
  34.6 1.0 %add_convert_fusion.1 = bf16[8,128,128]{2,1,0:T(8,128)(2,1)S(1)} fusion(f32[8,128,128]{2,1,0:T(8,128)S(1)} %get-tuple-element.24, bf16[8,128,128]{2,1,0:T(8,128)(2,1)} %collective-permute-done.5), kind=kLoop, calls=%fused_computation.3 | loop fusion | flops 393216 | bytes 1048576 | tf_op jit(solution)/shard_map/convert_element_type | solution.py:287
  35.6 1.7 %collective-permute-start.6 = (bf16[8,128,128]{2,1,0:T(8,128)(2,1)S(1)}, bf16[8,128,128]{2,1,0:T(8,128)(2,1)S(1)}, u32[]{:S(2)}, u32[]{:S(2)}) collective-permute-start(bf16[8,128,128]{2,1,0:T(8,128)(2,1)S(1)} %add_convert_fusion.1), channel_id=1, source_target_pairs={{0,2},{1,3},{2,0},{3,1},{4,6},{5,7},{6,4},{7,5},{8,10},{9,11},{10,... | collective-permute-start | bytes 786440 | tf_op jit(solution)/shard_map/ppermute | solution.py:253
  37.3 0.9 %add_convert_fusion.3 = bf16[2,128,128]{2,1,0:T(8,128)(2,1)S(1)} fusion(bf16[2,128,128]{2,1,0:T(8,128)(2,1)S(1)} %collective-permute-done.9, f32[8,128,128]{2,1,0:T(8,128)S(1)} %get-tuple-element.26, bf16[8,128,128]{2,1,0:T(8,128)(2,1)} %collective-permute-done.7), kind=kLoop, calls=%fused_computation.5 | loop fusion | flops 163840 | bytes 327680 | tf_op jit(solution)/shard_map/convert_element_type | solution.py:290
  38.1 2.7 %collective-permute-start.10 = (bf16[2,128,128]{2,1,0:T(8,128)(2,1)S(1)}, bf16[2,128,128]{2,1,0:T(8,128)(2,1)S(1)}, u32[]{:S(2)}, u32[]{:S(2)}) collective-permute-start(bf16[2,128,128]{2,1,0:T(8,128)(2,1)S(1)} %add_convert_fusion.3), channel_id=1, source_target_pairs={{0,4},{1,5},{2,6},{3,7},{4,0},{5,1},{6,2},{7,3},{8,12},{9,13},{10,... | collective-permute-start | bytes 196616 | tf_op jit(solution)/shard_map/ppermute | solution.py:253
  40.8 1.8 %collective-permute-done.11 = bf16[6,128,128]{2,1,0:T(8,128)(2,1)S(1)} collective-permute-done((bf16[6,128,128]{2,1,0:T(8,128)(2,1)S(1)}, bf16[6,128,128]{2,1,0:T(8,128)(2,1)S(1)}, u32[]{:S(2)}, u32[]{:S(2)}) %collective-permute-start.11) | collective-permute-done | bytes 196640 | tf_op jit(solution)/shard_map/ppermute | solution.py:253
  42.6 1.0 %add_convert_fusion.2 = bf16[6,128,128]{2,1,0:T(8,128)(2,1)S(1)} fusion(bf16[6,128,128]{2,1,0:T(8,128)(2,1)S(1)} %collective-permute-done.11, f32[8,128,128]{2,1,0:T(8,128)S(1)} %get-tuple-element.26, bf16[8,128,128]{2,1,0:T(8,128)(2,1)} %collective-permute-done.7), kind=kLoop, calls=%fused_computation.4 | loop fusion | flops 491520 | bytes 983040 | tf_op jit(solution)/shard_map/convert_element_type | solution.py:290
  43.6 2.0 %collective-permute-start.12 = (bf16[6,128,128]{2,1,0:T(8,128)(2,1)S(1)}, bf16[6,128,128]{2,1,0:T(8,128)(2,1)S(1)}, u32[]{:S(2)}, u32[]{:S(2)}) collective-permute-start(bf16[6,128,128]{2,1,0:T(8,128)(2,1)S(1)} %add_convert_fusion.2), channel_id=1, source_target_pairs={{0,4},{1,5},{2,6},{3,7},{4,0},{5,1},{6,2},{7,3},{8,12},{9,13},{10,... | collective-permute-start | bytes 589832 | tf_op jit(solution)/shard_map/ppermute | solution.py:253
  45.6 5.4 %collective-permute-done.6 = bf16[8,128,128]{2,1,0:T(8,128)(2,1)S(1)} collective-permute-done((bf16[8,128,128]{2,1,0:T(8,128)(2,1)S(1)}, bf16[8,128,128]{2,1,0:T(8,128)(2,1)S(1)}, u32[]{:S(2)}, u32[]{:S(2)}) %collective-permute-start.6) | collective-permute-done | bytes 262176 | tf_op jit(solution)/shard_map/ppermute | solution.py:253
  51.0 4.7 %collective-permute-done.12 = bf16[6,128,128]{2,1,0:T(8,128)(2,1)S(1)} collective-permute-done((bf16[6,128,128]{2,1,0:T(8,128)(2,1)S(1)}, bf16[6,128,128]{2,1,0:T(8,128)(2,1)S(1)}, u32[]{:S(2)}, u32[]{:S(2)}) %collective-permute-start.12) | collective-permute-done | bytes 196640 | tf_op jit(solution)/shard_map/ppermute | solution.py:253
  55.7 0.9 %multiply_bitcast_fusion = f32[1,8,128,128]{3,2,1,0:T(8,128)} fusion(f32[8,128,128]{2,1,0:T(8,128)S(1)} %convert_add_fusion, bf16[6,128,128]{2,1,0:T(8,128)(2,1)S(1)} %collective-permute-done.12, bf16[2,128,128]{2,1,0:T(8,128)(2,1)S(1)} %collective-permute-done.10), kind=kLoop, calls=%fused_computation | loop fusion | flops 524288 | bytes 1310720 | tf_op jit(solution)/shard_map/broadcast_in_dim | solution.py:305
  (27 shorter events, 1.1 us)
Async XLA Ops:
  5.8 15.2 %copy-start = (bf16[1,64,4096]{2,1,0:T(8,128)(2,1)S(1)}, bf16[1,64,4096]{2,1,0:T(8,128)(2,1)}, u32[]{:S(2)}) copy-start(bf16[1,64,4096]{2,1,0:T(8,128)(2,1)} %param.9) | copy-start | bytes 1572868
  5.8 15.2 %copy-start.5 = (s32[1,4,16]{2,1,0:T(4,128)S(1)}, s32[1,4,16]{2,1,0:T(4,128)}, u32[]{:S(2)}) copy-start(s32[1,4,16]{2,1,0:T(4,128)} %param.13) | copy-start | bytes 772
  5.8 9.5 %collective-permute-start = (bf16[64,1024]{1,0:T(8,128)(2,1)S(1)}, bf16[64,1024]{1,0:T(8,128)(2,1)S(1)}, u32[]{:S(2)}, u32[]{:S(2)}) collective-permute-start(bf16[64,1024]{1,0:T(8,128)(2,1)S(1)} %get-tuple-element.18), channel_id=1, source_target_pairs={{0,24},{8,0},{16,8},{24,16},{1,25},{9,1},{17,9},{25,17},{2,26},{10... | collective-permute-start | bytes 393224 | tf_op jit(solution)/shard_map/ppermute | solution.py:258
  9.8 6.7 %collective-permute-start.1 = (bf16[64,1024]{1,0:T(8,128)(2,1)S(1)}, bf16[64,1024]{1,0:T(8,128)(2,1)S(1)}, u32[]{:S(2)}, u32[]{:S(2)}) collective-permute-start(bf16[64,1024]{1,0:T(8,128)(2,1)S(1)} %get-tuple-element.19), channel_id=1, source_target_pairs={{0,24},{8,0},{16,8},{24,16},{1,25},{9,1},{17,9},{25,17},{2,26},{10... | collective-permute-start | bytes 393224 | tf_op jit(solution)/shard_map/ppermute | solution.py:258
  10.3 9.0 %collective-permute-start.2 = (bf16[64,1024]{1,0:T(8,128)(2,1)S(1)}, bf16[64,1024]{1,0:T(8,128)(2,1)S(1)}, u32[]{:S(2)}, u32[]{:S(2)}) collective-permute-start(bf16[64,1024]{1,0:T(8,128)(2,1)S(1)} %get-tuple-element.20), channel_id=1, source_target_pairs={{0,24},{8,0},{16,8},{24,16},{1,25},{9,1},{17,9},{25,17},{2,26},{10... | collective-permute-start | bytes 393224 | tf_op jit(solution)/shard_map/ppermute | solution.py:258
  11.7 9.2 %collective-permute-start.3 = (bf16[64,1024]{1,0:T(8,128)(2,1)S(1)}, bf16[64,1024]{1,0:T(8,128)(2,1)S(1)}, u32[]{:S(2)}, u32[]{:S(2)}) collective-permute-start(bf16[64,1024]{1,0:T(8,128)(2,1)S(1)} %get-tuple-element.21), channel_id=1, source_target_pairs={{0,24},{8,0},{16,8},{24,16},{1,25},{9,1},{17,9},{25,17},{2,26},{10... | collective-permute-start | bytes 393224 | tf_op jit(solution)/shard_map/ppermute | solution.py:258
  15.3 10.1 %copy-start.1 = (bf16[64,1024]{1,0:T(8,128)(2,1)}, bf16[64,1024]{1,0:T(8,128)(2,1)S(1)}, u32[]{:S(2)}) copy-start(bf16[64,1024]{1,0:T(8,128)(2,1)S(1)} %collective-permute-done.refs_0_) | copy-start | bytes 393220
  16.5 8.9 %copy-start.2 = (bf16[64,1024]{1,0:T(8,128)(2,1)}, bf16[64,1024]{1,0:T(8,128)(2,1)S(1)}, u32[]{:S(2)}) copy-start(bf16[64,1024]{1,0:T(8,128)(2,1)S(1)} %collective-permute-done.1.refs_1_) | copy-start | bytes 393220
  19.3 6.1 %copy-start.3 = (bf16[64,1024]{1,0:T(8,128)(2,1)}, bf16[64,1024]{1,0:T(8,128)(2,1)S(1)}, u32[]{:S(2)}) copy-start(bf16[64,1024]{1,0:T(8,128)(2,1)S(1)} %collective-permute-done.2.refs_2_) | copy-start | bytes 393220
  20.9 4.5 %copy-start.4 = (bf16[64,1024]{1,0:T(8,128)(2,1)}, bf16[64,1024]{1,0:T(8,128)(2,1)S(1)}, u32[]{:S(2)}) copy-start(bf16[64,1024]{1,0:T(8,128)(2,1)S(1)} %collective-permute-done.3.refs_3_) | copy-start | bytes 393220
  22.5 8.9 %collective-permute-start.8 = (bf16[8,128,128]{2,1,0:T(8,128)(2,1)}, bf16[8,128,128]{2,1,0:T(8,128)(2,1)}, u32[]{:S(2)}, u32[]{:S(2)}) collective-permute-start(bf16[8,128,128]{2,1,0:T(8,128)(2,1)} %get-tuple-element.29), channel_id=1, source_target_pairs={{0,1},{1,0},{2,3},{3,2},{4,5},{5,4},{6,7},{7,6},{8,9},{9,8},{10,11... | collective-permute-start | bytes 786440 | tf_op jit(solution)/shard_map/ppermute | solution.py:253
  24.4 12.9 %collective-permute-start.7 = (bf16[8,128,128]{2,1,0:T(8,128)(2,1)S(1)}, bf16[8,128,128]{2,1,0:T(8,128)(2,1)}, u32[]{:S(2)}, u32[]{:S(2)}) collective-permute-start(bf16[8,128,128]{2,1,0:T(8,128)(2,1)S(1)} %get-tuple-element.27), channel_id=1, source_target_pairs={{0,1},{1,0},{2,3},{3,2},{4,5},{5,4},{6,7},{7,6},{8,9},{9,8},{10,11... | collective-permute-start | bytes 786440 | tf_op jit(solution)/shard_map/ppermute | solution.py:253
  24.9 9.7 %collective-permute-start.5 = (bf16[8,128,128]{2,1,0:T(8,128)(2,1)}, bf16[8,128,128]{2,1,0:T(8,128)(2,1)}, u32[]{:S(2)}, u32[]{:S(2)}) collective-permute-start(bf16[8,128,128]{2,1,0:T(8,128)(2,1)} %get-tuple-element.25), channel_id=1, source_target_pairs={{0,1},{1,0},{2,3},{3,2},{4,5},{5,4},{6,7},{7,6},{8,9},{9,8},{10,11... | collective-permute-start | bytes 786440 | tf_op jit(solution)/shard_map/ppermute | solution.py:253
  24.9 20.7 %collective-permute-start.4 = (bf16[8,128,128]{2,1,0:T(8,128)(2,1)S(1)}, bf16[8,128,128]{2,1,0:T(8,128)(2,1)S(1)}, u32[]{:S(2)}, u32[]{:S(2)}) collective-permute-start(bf16[8,128,128]{2,1,0:T(8,128)(2,1)S(1)} %get-tuple-element.23), channel_id=1, source_target_pairs={{0,1},{1,0},{2,3},{3,2},{4,5},{5,4},{6,7},{7,6},{8,9},{9,8},{10,11... | collective-permute-start | bytes 786440 | tf_op jit(solution)/shard_map/ppermute | solution.py:253
  32.5 4.8 %collective-permute-start.9 = (bf16[2,128,128]{2,1,0:T(8,128)(2,1)S(1)}, bf16[2,128,128]{2,1,0:T(8,128)(2,1)S(1)}, u32[]{:S(2)}, u32[]{:S(2)}) collective-permute-start(bf16[2,128,128]{2,1,0:T(8,128)(2,1)S(1)} %slice.25), channel_id=1, source_target_pairs={{0,2},{1,3},{2,0},{3,1},{4,6},{5,7},{6,4},{7,5},{8,10},{9,11},{10,... | collective-permute-start | bytes 196616 | tf_op jit(solution)/shard_map/ppermute | solution.py:253
  34.2 8.5 %collective-permute-start.11 = (bf16[6,128,128]{2,1,0:T(8,128)(2,1)S(1)}, bf16[6,128,128]{2,1,0:T(8,128)(2,1)S(1)}, u32[]{:S(2)}, u32[]{:S(2)}) collective-permute-start(bf16[6,128,128]{2,1,0:T(8,128)(2,1)S(1)} %slice.27), channel_id=1, source_target_pairs={{0,2},{1,3},{2,0},{3,1},{4,6},{5,7},{6,4},{7,5},{8,10},{9,11},{10,... | collective-permute-start | bytes 589832 | tf_op jit(solution)/shard_map/ppermute | solution.py:253
  35.6 15.4 %collective-permute-start.6 = (bf16[8,128,128]{2,1,0:T(8,128)(2,1)S(1)}, bf16[8,128,128]{2,1,0:T(8,128)(2,1)S(1)}, u32[]{:S(2)}, u32[]{:S(2)}) collective-permute-start(bf16[8,128,128]{2,1,0:T(8,128)(2,1)S(1)} %add_convert_fusion.1), channel_id=1, source_target_pairs={{0,2},{1,3},{2,0},{3,1},{4,6},{5,7},{6,4},{7,5},{8,10},{9,11},{10,... | collective-permute-start | bytes 786440 | tf_op jit(solution)/shard_map/ppermute | solution.py:253
  38.1 12.9 %collective-permute-start.10 = (bf16[2,128,128]{2,1,0:T(8,128)(2,1)S(1)}, bf16[2,128,128]{2,1,0:T(8,128)(2,1)S(1)}, u32[]{:S(2)}, u32[]{:S(2)}) collective-permute-start(bf16[2,128,128]{2,1,0:T(8,128)(2,1)S(1)} %add_convert_fusion.3), channel_id=1, source_target_pairs={{0,4},{1,5},{2,6},{3,7},{4,0},{5,1},{6,2},{7,3},{8,12},{9,13},{10,... | collective-permute-start | bytes 196616 | tf_op jit(solution)/shard_map/ppermute | solution.py:253
  43.6 12.1 %collective-permute-start.12 = (bf16[6,128,128]{2,1,0:T(8,128)(2,1)S(1)}, bf16[6,128,128]{2,1,0:T(8,128)(2,1)S(1)}, u32[]{:S(2)}, u32[]{:S(2)}) collective-permute-start(bf16[6,128,128]{2,1,0:T(8,128)(2,1)S(1)} %add_convert_fusion.2), channel_id=1, source_target_pairs={{0,4},{1,5},{2,6},{3,7},{4,0},{5,1},{6,2},{7,3},{8,12},{9,13},{10,... | collective-permute-start | bytes 589832 | tf_op jit(solution)/shard_map/ppermute | solution.py:253

commit v4 on v3

v4 whole, which is shorter than its diff:
```python
import functools

import jax
import jax.numpy as jnp
from jax import lax
from jax.experimental import pallas as pl
from jax.experimental.pallas import tpu as pltpu
from jax.sharding import PartitionSpec as P


F32 = jnp.float32
BF16 = jnp.bfloat16
NT = (((1,), (1,)), ((), ()))
NN = (((1,), (0,)), ((), ()))
VMEM = pl.BlockSpec(memory_space=pltpu.VMEM)
SMEM = pl.BlockSpec(memory_space=pltpu.SMEM)
HBM = pl.BlockSpec(memory_space=pl.ANY)
ROOM = pltpu.CompilerParams(vmem_limit_bytes=16 << 20)
FULL = pltpu.CompilerParams(vmem_limit_bytes=60 * 1024 * 1024)


def cost(flops, nbytes):
    return pl.CostEstimate(flops=flops, bytes_accessed=nbytes, transcendentals=0)


def block(ref, index, size):
    return ref[:, pl.ds(pl.multiple_of(index * size, size), size)]


def pairs(keep):
    return [(j, j + 1) for j in range(0, keep, 2)]


def hidden_grad(ok, g, o, c):
    keep, size = o.shape[1], o.shape[2]
    total = None
    for both in pairs(keep):
        left = jnp.concatenate([block(g, ok[c, j], size) for j in both], axis=1)
        right = jnp.concatenate([o[c, j] for j in both], axis=1)
        term = lax.dot_general(left, right, NT, preferred_element_type=F32)
        total = term if total is None else total + term
    return total.astype(BF16)


def add_back(vk, hidden, v, c, acc, first=0):
    keep, size = v.shape[1], v.shape[2]
    for both in pairs(keep):
        right = jnp.concatenate([v[c, j] for j in both], axis=0)
        term = lax.dot_general(hidden, right, NT, preferred_element_type=F32)
        for i, j in enumerate(both):
            cols = pl.ds(pl.multiple_of(vk[c, first + j] * size, size), size)
            acc[:, cols] = acc[:, cols] + term[:, i * size:(i + 1) * size]


def first_kernel(vk_hbm, ok_hbm, g_hbm, o_hbm, v_hbm, *refs):
    (chunk, acc, hidden, v_high, vk), (g, o, v_low, ok, sem, w_sem) = refs[:5], refs[5:]
    kvb, low, keep = o.shape[0], v_low.shape[1], v_hbm.shape[1]
    copy = pltpu.make_async_copy
    small = [copy(ok_hbm, ok, sem.at[0]), copy(g_hbm, g, sem.at[1]), copy(vk_hbm, vk, sem.at[2])]
    o_copies = [copy(o_hbm.at[c], o.at[c], w_sem.at[0, c]) for c in range(kvb)]
    v_copies = [copy(v_hbm.at[c, pl.ds(0, low)], v_low.at[c], w_sem.at[1, c]) for c in range(kvb)]
    rest = [copy(v_hbm.at[c, pl.ds(low, keep - low)], v_high.at[c], w_sem.at[2, c]) for c in range(kvb)]
    for each in small + o_copies:
        each.start()
    small[0].wait()
    small[1].wait()
    acc[...] = g[...].astype(F32)
    for c in range(kvb):
        o_copies[c].wait()
        v_copies[c].start()
        if c == kvb - 1:
            for each in rest:
                each.start()
        hidden[c] = hidden_grad(ok, g, o, c)
    small[2].wait()
    for c in range(kvb):
        v_copies[c].wait()
        add_back(vk, hidden[c], v_low, c, acc)
    chunk[...] = acc[:, :chunk.shape[1]].astype(BF16)
    for each in rest:
        each.wait()


def first_call(g, w_value, w_output, value_idx, output_idx, wide):
    tokens, width = g.shape
    kvb, keep, size, _ = w_value.shape
    low = wide // size
    return pl.pallas_call(
        first_kernel,
        out_shape=[
            pltpu.VMEM((tokens, wide), BF16),
            pltpu.VMEM((tokens, width), F32),
            pltpu.VMEM((kvb, tokens, size), BF16),
            pltpu.VMEM((kvb, keep - low, size, size), BF16),
            pltpu.SMEM(value_idx.shape, jnp.int32),
        ],
        in_specs=[HBM] * 5,
        out_specs=[VMEM] * 4 + [SMEM],
        scratch_shapes=[
            pltpu.VMEM((tokens, width), BF16),
            pltpu.VMEM(w_output.shape, BF16),
            pltpu.VMEM((kvb, low, size, size), BF16),
            pltpu.SMEM(output_idx.shape, jnp.int32),
            pltpu.SemaphoreType.DMA((3,)),
            pltpu.SemaphoreType.DMA((3, kvb)),
        ],
        compiler_params=FULL,
        cost_estimate=cost(3 * tokens * kvb * keep * size * size, 5 << 20),
        name="first",
    )(value_idx, output_idx, g, w_output, w_value)


def rest_kernel(vk, hidden, v_high, acc_in, acc, *outs):
    kvb, high = v_high.shape[0], v_high.shape[1]
    for c in range(kvb):
        add_back(vk, hidden[c], v_high, c, acc, vk.shape[1] - high)
    at = acc.shape[1] - sum(out.shape[1] for out in outs)
    for out in outs:
        wide = out.shape[1]
        out[...] = acc[:, at:at + wide].astype(BF16)
        at += wide


def rest_call(value_idx, hidden, v_high, acc, widths):
    tokens = acc.shape[0]
    return pl.pallas_call(
        rest_kernel,
        out_shape=[pltpu.VMEM(acc.shape, F32)] + [pltpu.VMEM((tokens, w), BF16) for w in widths],
        in_specs=[SMEM] + [VMEM] * 3,
        out_specs=[VMEM] * (1 + len(widths)),
        input_output_aliases={3: 0},
        compiler_params=ROOM,
        cost_estimate=cost(2 * tokens * v_high.size, 2 << 20),
        name="rest",
    )(value_idx, hidden, v_high, acc)[1:]


def fetch(sources, targets, sem):
    copies = [pltpu.make_async_copy(a, b, sem.at[i]) for i, (a, b) in enumerate(zip(sources, targets))]
    for copy in copies:
        copy.start()
    return copies


def second_kernel(vk_hbm, ok_hbm, o_hbm, v_hbm, stack, out, o, v, acc, vk, ok, sem):
    kvb = o.shape[0]
    both = [r.at[c] for r in (o_hbm, v_hbm) for c in range(kvb)]
    into = [r.at[c] for r in (o, v) for c in range(kvb)]
    copies = fetch([ok_hbm, vk_hbm] + both, [ok, vk] + into, sem)
    tokens = acc.shape[0]
    g = stack.at[pl.ds(tokens, tokens)]
    acc[...] = g[...].astype(F32)
    copies[0].wait()
    hidden = []
    for c in range(kvb):
        copies[2 + c].wait()
        hidden.append(hidden_grad(ok, g, o, c))
    copies[1].wait()
    for c in range(kvb):
        copies[2 + kvb + c].wait()
        add_back(vk, hidden[c], v, c, acc)
    out[...] = acc[...].astype(BF16)


def second_call(stack, w_value, w_output, value_idx, output_idx):
    tokens, width = stack.shape[0] // 2, stack.shape[1]
    kvb, keep, size, _ = w_value.shape
    return pl.pallas_call(
        second_kernel,
        out_shape=jax.ShapeDtypeStruct((tokens, width), BF16),
        in_specs=[HBM] * 4 + [VMEM],
        out_specs=VMEM,
        scratch_shapes=[
            pltpu.VMEM(w_output.shape, BF16),
            pltpu.VMEM(w_value.shape, BF16),
            pltpu.VMEM((tokens, width), F32),
            pltpu.SMEM(value_idx.shape, jnp.int32),
            pltpu.SMEM(output_idx.shape, jnp.int32),
            pltpu.SemaphoreType.DMA((2 + 2 * kvb,)),
        ],
        compiler_params=FULL,
        cost_estimate=cost(4 * tokens * kvb * keep * size * size, 5 << 20),
        name="second",
    )(value_idx, output_idx, w_output, w_value, stack)


def hidden_kernel(vk, x1, x2, v_hbm, out, x, v, sem):
    tokens = x1.shape[0]
    kvb, keep, size, _ = v.shape
    copies = fetch(
        [x1, x2] + [v_hbm.at[c] for c in range(kvb)],
        [x.at[pl.ds(0, tokens)], x.at[pl.ds(tokens, tokens)]] + [v.at[c] for c in range(kvb)],
        sem,
    )
    copies[0].wait()
    copies[1].wait()
    for c in range(kvb):
        copies[2 + c].wait()
        total = None
        for both in pairs(keep):
            left = jnp.concatenate([block(x, vk[c, j], size) for j in both], axis=1)
            right = jnp.concatenate([v[c, j] for j in both], axis=0)
            term = lax.dot_general(left, right, NN, preferred_element_type=F32)
            total = term if total is None else total + term
        out[c] = total.astype(BF16).T


def hidden_call(x1, x2, w_value, value_idx):
    tokens, width = x1.shape
    kvb, keep, size, _ = w_value.shape
    return pl.pallas_call(
        hidden_kernel,
        out_shape=pltpu.VMEM((kvb, size, 2 * tokens), BF16),
        in_specs=[SMEM, HBM, HBM, HBM],
        out_specs=VMEM,
        scratch_shapes=[
            pltpu.VMEM((2 * tokens, width), BF16),
            pltpu.VMEM(w_value.shape, BF16),
            pltpu.SemaphoreType.DMA((2 + kvb,)),
        ],
        compiler_params=FULL,
        cost_estimate=cost(4 * tokens * kvb * keep * size * size, 3 << 20),
        name="hidden",
    )(value_idx, x1, x2, w_value)


def reverse_bits(value, bits):
    out = 0
    for _ in range(bits):
        out, value = out * 2 + value % 2, value // 2
    return out


def stack_kernel(ok, me, g, *refs):
    parts, (stack, ok_out, me_out) = refs[:-3], refs[-3:]
    me_out[0] = me[0]
    for c in range(ok.shape[0]):
        for j in range(ok.shape[1]):
            ok_out[c, j] = ok[c, j]
    tokens = g.shape[0]
    stack[:tokens] = g[...]
    at = 0
    for part in parts:
        wide = part.shape[1]
        stack[tokens:, at:at + wide] = part[...]
        at += wide


def stack_call(output_idx, me, g, parts):
    tokens, width = g.shape
    return pl.pallas_call(
        stack_kernel,
        out_shape=[
            pltpu.VMEM((2 * tokens, width), BF16),
            pltpu.SMEM(output_idx.shape, jnp.int32),
            pltpu.SMEM(me.shape, jnp.int32),
        ],
        in_specs=[SMEM, SMEM] + [VMEM] * (1 + len(parts)),
        out_specs=[VMEM, SMEM, SMEM],
        compiler_params=ROOM,
        cost_estimate=cost(0, 1 << 20),
        name="stack",
    )(output_idx, me, g, *parts)


def tile_kernel(per, bits, starts, me, ok, h, stack, *refs):
    outs = refs[-len(starts):]
    size = h.shape[1]
    keep = ok.shape[1]
    if len(refs) > len(starts):
        part, stack = refs[0], refs[1]
        tokens, wide = part.shape
        stack[tokens:, stack.shape[1] - wide:] = part[...]
    flip = me[0] * per
    for out, start in zip(outs, starts):
        for i in range(out.shape[0]):
            position = start + i
            tile = (reverse_bits(position // per, bits) * per + position % per) ^ flip
            c, j = tile // keep, lax.rem(tile, keep)
            term = lax.dot_general(h[c], block(stack, ok[c, j], size), NN, preferred_element_type=F32)
            out[i] = term.astype(out.dtype)


def tile_call(runs, me, output_idx, hidden, stack, ranks, part=()):
    kvb, size, stacked = hidden.shape
    keep = output_idx.shape[1]
    total = kvb * keep
    count = sum(n for _, n, _ in runs)
    outs = [pltpu.VMEM((n, size, size), kind) for _, n, kind in runs]
    if part:
        outs = [pltpu.VMEM(stack.shape, BF16)] + outs
    return pl.pallas_call(
        functools.partial(
            tile_kernel, total // ranks, ranks.bit_length() - 1, [start for start, _, _ in runs]
        ),
        out_shape=outs,
        in_specs=[SMEM, SMEM] + [VMEM] * (2 + len(part)),
        out_specs=[VMEM] * len(outs),
        input_output_aliases={3: 0} if part else {},
        compiler_params=ROOM,
        cost_estimate=cost(2 * stacked * count * size * size, 2 << 20),
        name="tiles",
    )(me, output_idx, hidden, stack, *part)


def exchange(value, axis, bit):
    count = lax.axis_size(axis)
    return lax.ppermute(value, axis, [(i, i ^ bit) for i in range(count)])


def from_behind(value, axis, steps):
    count = lax.axis_size(axis)
    return lax.ppermute(value, axis, [(i, (i + steps) % count) for i in range(count)])


def per_device(x_first, x_second, grad_first, value_tiles, output_tiles, value_keep, output_keep):
    w_value, w_output = value_tiles[0], output_tiles[0]
    value_idx, output_idx = value_keep[0], output_keep[0]
    g = grad_first[0]
    width = g.shape[1]
    ranks = lax.axis_size("dp")
    me = lax.axis_index("dp").astype(jnp.int32).reshape(1)
    parts = 4
    wide = width // parts
    chunk, acc, down, v_high, vk = first_call(g, w_value, w_output, value_idx, output_idx, wide)
    arrived = [from_behind(chunk, "section", -1)]
    others = rest_call(vk, down, v_high, acc, [wide] * (parts - 1))
    for part in others:
        arrived.append(from_behind(part, "section", -1))
    hidden = hidden_call(x_first[0], x_second[0], w_value, value_idx)
    run = w_value.shape[0] * w_value.shape[1] // 8
    at = {"kd": 0, "kc": 1, "kb": 2, "ka": 3, "sd": 4, "sc": 5, "sb": 6, "sa": 7}
    stack, kept_idx, me = stack_call(output_idx, me, g, arrived[:-1])
    tiles = functools.partial(
        tile_call, me=me, output_idx=kept_idx, hidden=hidden, ranks=ranks
    )
    spec = lambda *names: [(at[n] * run, run, BF16 if n[0] == "s" else F32) for n in names]
    few = run // 4
    first_tiles = [(at["sa"] * run, few, BF16), (at["sa"] * run + few, run - few, BF16)]
    stack, sa0, sa1, ka = tiles(first_tiles + spec("ka"), stack=stack, part=arrived[-1:])
    got_a = []
    for part in (sa0, sa1):
        got_a.append(exchange(part, "dp", 1))
    sc, kc = tiles(spec("sc", "kc"), stack=stack)
    got_c = exchange(sc, "dp", 1)
    sb, sd, kb, kd = tiles(spec("sb", "sd", "kb", "kd"), stack=stack)
    got_b, got_d = (exchange(s, "dp", 1) for s in (sb, sd))
    cuts = [slice(0, few), slice(few, run)]
    near = []
    for i, cut in enumerate(cuts):
        near.append(exchange((ka[cut] + got_a[i].astype(F32)).astype(BF16), "dp", 2))
        if i == 0:
            got_a[1], _ = lax.optimization_barrier((got_a[1], got_a[0]))
    near_b = exchange((kb + got_b.astype(F32)).astype(BF16), "dp", 2)
    far = []
    for i, cut in enumerate(cuts):
        out_c = (kc[cut] + got_c[cut].astype(F32) + near[i].astype(F32)).astype(BF16)
        if i == 0:
            near[1], _ = lax.optimization_barrier((near[1], out_c))
        far.append(exchange(out_c, "dp", 4))
    second = second_call(stack, w_value, w_output, value_idx, output_idx)
    staying = kd + got_d.astype(F32) + near_b.astype(F32)
    staying, far = lax.optimization_barrier((staying, far))
    staying = staying + jnp.concatenate(far, axis=0).astype(F32)
    bit = 8
    while bit < ranks:
        half = staying.shape[0] // 2
        came = exchange(staying[half:].astype(BF16), "dp", bit)
        staying = staying[:half] + came.astype(F32)
        bit *= 2
    weight_grad = staying * (1.0 / (2.0 * ranks))
    return second[None], weight_grad[None]


def solution(mesh):
    in_specs = (
        P("section", "dp", None),
        P("section", "dp", None),
        P("section", "dp", None),
        P("section", None, None, None, None),
        P("section", None, None, None, None),
        P("section", None, None),
        P("section", None, None),
    )
    out_specs = (P("section", "dp", None), P("section", "dp", None, None))

    return jax.shard_map(
        per_device, mesh=mesh, in_specs=in_specs, out_specs=out_specs, check_vma=False
    )
```

time: 56.9 us -> 56.3 us (0.989)
  other arithmetic: 4.81 us -> 6.59 us
  waiting for transfers between devices: 17.5 us -> 16 us
  Pallas kernels: 18.1 us -> 16.8 us
    pallas_call x2 -> x3, Pallas kernels: 3.42 us -> 1.76 us  [tile_call(): pl.pallas_call(functools.partial(tile_kernel, total // ranks, ranks.bit_l...]
    add x1, other arithmetic: 0.07 us -> 1.02 us  [per_device(): staying = kd + got_d.astype(F32) + near_b.astype(F32)]
    ppermute x9 -> x10, waiting for transfers between devices: 11.9 us -> 11 us  [exchange(): return lax.ppermute(value, axis, [(i, i ^ bit) for i in range(count)])]
    convert_element_type x1 -> x2, other arithmetic: 1.01 us -> 1.83 us  [per_device(): (ka[cut] + got_a[i].astype(F32)).astype(BF16)]
    ppermute x4, waiting for transfers between devices: 5.59 us -> 4.96 us  [from_behind(): lax.ppermute(value, axis, [(i, (i + steps) % count) for i in range(count)])]
    pallas_call x2 -> x4, Pallas kernels: 11.1 us -> 11.6 us  [the longest x1 6.12 us: second_call(): pl.pallas_call(second_kernel, out_shape=jax.ShapeDtypeStruct((tokens, wid...]
    ppermute x9 -> x10, starting transfers between devices: 9.42 us -> 9.64 us  [exchange(): return lax.ppermute(value, axis, [(i, i ^ bit) for i in range(count)])]
  transfers between devices with their start and end apart: 13 -> 14, of which waited for: 6 -> 6; matrix products, arithmetic and copies ran while one was open for 7% -> 10% of each run, Pallas kernels for 20% -> 20%
where the time goes in v4:
time: 56.3 us; the launch traced here: 55.8 us
  Pallas kernels  16.8 us (30%)
  waiting for transfers between devices  16 us (28%)
  starting transfers between devices  15.6 us (28%)
  other arithmetic  6.59 us (12%)
  between operations  0.76 us (1%)
    ppermute x10, waiting for transfers between devices, exchange(): return lax.ppermute(value, axis, [(i, i ^ bit) for i in range(count)])  11 us
    ppermute x10, starting transfers between devices, exchange(): return lax.ppermute(value, axis, [(i, i ^ bit) for i in range(count)])  9.64 us
    pallas_call x1, Pallas kernels, second_call(): pl.pallas_call(second_kernel, out_shape=jax.ShapeDtypeStruct((tokens, wid...  6.12 us
    ppermute x4, starting transfers between devices, from_behind(): lax.ppermute(value, axis, [(i, (i + steps) % count) for i in range(count)])  6 us
    ppermute x4, waiting for transfers between devices, from_behind(): lax.ppermute(value, axis, [(i, (i + steps) % count) for i in range(count)])  4.96 us
    pallas_call x1, Pallas kernels, first_call(): pl.pallas_call(first_kernel, out_shape=[pltpu.VMEM((tokens, wide), BF16),...  4.25 us
    pallas_call x1, Pallas kernels, hidden_call(): pl.pallas_call(hidden_kernel, out_shape=pltpu.VMEM((kvb, size, 2 * tokens...  3.53 us
    convert_element_type x2, other arithmetic, per_device(): (kc[cut] + got_c[cut].astype(F32) + near[i].astype(F32)).astype(BF16)  1.87 us
  transfers between devices with their start and end apart: 14, of which 6 were waited for; matrix products, arithmetic and copies ran while one was open for 10% of the time, Pallas kernels for 20%

profile of v4, /device:TPU:0, one launch (start us, length us, event | category | flops | bytes accessed | tf_op | source)
XLA Modules:
  0.0 55.8 jit_solution(10996235885170864396)
XLA Ops:
  0.6 4.2 %first.1 = (bf16[64,1024]{1,0:T(8,128)(2,1)S(1)}, f32[64,4096]{1,0:T(8,128)S(1)}, bf16[4,64,128]{2,1,0:T(8,128)(2,1)S(1)}, bf16[4,8,128,128]{3,2,1,0:T(8,128)(2,1)S(1)}, s32[4,16]{1,0:T(4,128)S(4)}) custom-call(s32[4,16]{1,0:T(4,128)} %bitcast.24, s32[4,16]{1,0:T(4,128)} %bitcast.13, bf16[64,4096]{1,0:T(8,128)(2,1)} %bitcast.11, ...), custom_call_target="tpu_custom_call" | custom-call | flops 201326592 | bytes 5242880 | tf_op jit(solution)/shard_map/first/pallas_call | solution.py:88
  5.5 4.0 %collective-permute-start.1 = (bf16[64,1024]{1,0:T(8,128)(2,1)S(1)}, bf16[64,1024]{1,0:T(8,128)(2,1)S(1)}, u32[]{:S(2)}, u32[]{:S(2)}) collective-permute-start(bf16[64,1024]{1,0:T(8,128)(2,1)S(1)} %get-tuple-element.33), channel_id=1, source_target_pairs={{0,24},{8,0},{16,8},{24,16},{1,25},{9,1},{17,9},{25,17},{2,26},{10... | collective-permute-start | bytes 393224 | tf_op jit(solution)/shard_map/ppermute | solution.py:313
  10.0 1.4 %collective-permute-start = (bf16[64,1024]{1,0:T(8,128)(2,1)S(1)}, bf16[64,1024]{1,0:T(8,128)(2,1)S(1)}, u32[]{:S(2)}, u32[]{:S(2)}) collective-permute-start(bf16[64,1024]{1,0:T(8,128)(2,1)S(1)} %get-tuple-element.28), channel_id=1, source_target_pairs={{0,24},{8,0},{16,8},{24,16},{1,25},{9,1},{17,9},{25,17},{2,26},{10... | collective-permute-start | bytes 393224 | tf_op jit(solution)/shard_map/ppermute | solution.py:313
  11.5 3.5 %hidden.1.h = bf16[4,128,128]{2,1,0:T(8,128)(2,1)S(1)} custom-call(s32[4,16]{1,0:T(4,128)} %bitcast.25, bf16[64,4096]{1,0:T(8,128)(2,1)} %bitcast.22, bf16[64,4096]{1,0:T(8,128)(2,1)} %bitcast.23, bf16[4,16,128,128]{3,2,1,0:T(8,128)(2,1)} %bitcast.17), custom_call_target="tpu_custom_call" | custom-call | flops 268435456 | bytes 3145728 | tf_op jit(solution)/shard_map/hidden/pallas_call | solution.py:211
  15.0 1.1 %collective-permute-done.2.refs_2_ = bf16[64,1024]{1,0:T(8,128)(2,1)S(1)} collective-permute-done((bf16[64,1024]{1,0:T(8,128)(2,1)S(1)}, bf16[64,1024]{1,0:T(8,128)(2,1)S(1)}, u32[]{:S(2)}, u32[]{:S(2)}) %collective-permute-start.2) | collective-permute-done | bytes 131104 | tf_op jit(solution)/shard_map/ppermute | solution.py:313
  16.2 2.8 %collective-permute-done.refs_0_ = bf16[64,1024]{1,0:T(8,128)(2,1)S(1)} collective-permute-done((bf16[64,1024]{1,0:T(8,128)(2,1)S(1)}, bf16[64,1024]{1,0:T(8,128)(2,1)S(1)}, u32[]{:S(2)}, u32[]{:S(2)}) %collective-permute-start) | collective-permute-done | bytes 131104 | tf_op jit(solution)/shard_map/ppermute | solution.py:313
  19.0 0.6 %stack.1 = (bf16[128,4096]{1,0:T(8,128)(2,1)S(1)}, s32[4,16]{1,0:T(4,128)S(4)}, s32[1]{0:T(128)S(4)}) custom-call(s32[4,16]{1,0:T(4,128)S(1)} %bitcast.15, s32[1]{0:T(128)} %bitcast.4.me, bf16[64,4096]{1,0:T(8,128)(2,1)S(1)} %bitcast.12, bf16[64,1024]{1,0:T(8,128)(2,1)S(1)} %collective-permute-done.refs_0_, ...), custom_call_target="tpu_custom_call" | custom-call | bytes 1048576 | tf_op jit(solution)/shard_map/stack/pallas_call | solution.py:251
  19.6 1.0 %collective-permute-done.3.refs_0_ = bf16[64,1024]{1,0:T(8,128)(2,1)S(1)} collective-permute-done((bf16[64,1024]{1,0:T(8,128)(2,1)S(1)}, bf16[64,1024]{1,0:T(8,128)(2,1)S(1)}, u32[]{:S(2)}, u32[]{:S(2)}) %collective-permute-start.3) | collective-permute-done | bytes 131104 | tf_op jit(solution)/shard_map/ppermute | solution.py:313
  20.6 0.9 %tiles.3 = (bf16[128,4096]{1,0:T(8,128)(2,1)S(1)}, bf16[2,128,128]{2,1,0:T(8,128)(2,1)S(1)}, bf16[6,128,128]{2,1,0:T(8,128)(2,1)}, f32[8,128,128]{2,1,0:T(8,128)S(1)}) custom-call(s32[1]{0:T(128)S(4)} %get-tuple-element.35.me, s32[4,16]{1,0:T(4,128)S(4)} %get-tuple-element.36.ok, bf16[4,128,128]{2,1,0:T(8,128)(2,1)S(1)} %hidden.1.h, ...), custom_call_target="tpu_custom_call", output_to_operand_aliasing={{0}: (3, {})} | custom-call | flops 67108864 | bytes 2097152 | tf_op jit(solution)/shard_map/tiles/pallas_call | solution.py:292
  23.6 6.1 %second.1 = bf16[64,4096]{1,0:T(8,128)(2,1)} custom-call(s32[4,16]{1,0:T(4,128)} %bitcast.26, s32[4,16]{1,0:T(4,128)} %bitcast.14, bf16[4,16,128,128]{3,2,1,0:T(8,128)(2,1)} %bitcast.20, bf16[4,16,128,128]{3,2,1,0:T(8,128)(2,1)} %bitcast.18, bf16[128,4096]{1,0:T(8,128)(2,1)} %copy-done), custom_call_target="tpu_custom_call" | custom-call | flops 268435456 | bytes 5242880 | tf_op jit(solution)/shard_map/second/pallas_call | solution.py:168
  29.8 0.9 %add_convert_fusion.4 = bf16[2,128,128]{2,1,0:T(8,128)(2,1)S(1)} fusion(bf16[2,128,128]{2,1,0:T(8,128)(2,1)} %collective-permute-done.8, f32[8,128,128]{2,1,0:T(8,128)S(1)} %get-tuple-element.46), kind=kLoop, calls=%fused_computation.6 | loop fusion | flops 98304 | bytes 262144 | tf_op jit(solution)/shard_map/convert_element_type | solution.py:351
  30.6 1.7 %collective-permute-start.9 = (bf16[2,128,128]{2,1,0:T(8,128)(2,1)S(1)}, bf16[2,128,128]{2,1,0:T(8,128)(2,1)S(1)}, u32[]{:S(2)}, u32[]{:S(2)}) collective-permute-start(bf16[2,128,128]{2,1,0:T(8,128)(2,1)S(1)} %add_convert_fusion.4), channel_id=1, source_target_pairs={{0,2},{1,3},{2,0},{3,1},{4,6},{5,7},{6,4},{7,5},{8,10},{9,11},{10,... | collective-permute-start | bytes 196616 | tf_op jit(solution)/shard_map/ppermute | solution.py:308
  32.3 1.0 %add_convert_fusion.2 = bf16[6,128,128]{2,1,0:T(8,128)(2,1)S(1)} fusion(bf16[6,128,128]{2,1,0:T(8,128)(2,1)} %collective-permute-done.11, f32[8,128,128]{2,1,0:T(8,128)S(1)} %get-tuple-element.46), kind=kLoop, calls=%fused_computation.4 | loop fusion | flops 294912 | bytes 786432 | tf_op jit(solution)/shard_map/convert_element_type | solution.py:351
  33.7 1.0 %add_convert_fusion = bf16[8,128,128]{2,1,0:T(8,128)(2,1)S(1)} fusion(f32[8,128,128]{2,1,0:T(8,128)S(1)} %get-tuple-element.42, bf16[8,128,128]{2,1,0:T(8,128)(2,1)} %collective-permute-done.5), kind=kLoop, calls=%fused_computation.2 | loop fusion | flops 393216 | bytes 1048576 | tf_op jit(solution)/shard_map/convert_element_type | solution.py:354
  34.8 1.7 %collective-permute-start.6 = (bf16[8,128,128]{2,1,0:T(8,128)(2,1)S(1)}, bf16[8,128,128]{2,1,0:T(8,128)(2,1)S(1)}, u32[]{:S(2)}, u32[]{:S(2)}) collective-permute-start(bf16[8,128,128]{2,1,0:T(8,128)(2,1)S(1)} %add_convert_fusion), channel_id=1, source_target_pairs={{0,2},{1,3},{2,0},{3,1},{4,6},{5,7},{6,4},{7,5},{8,10},{9,11},{10,... | collective-permute-start | bytes 786440 | tf_op jit(solution)/shard_map/ppermute | solution.py:308
  36.4 0.9 %add_convert_fusion.3 = bf16[2,128,128]{2,1,0:T(8,128)(2,1)S(1)} fusion(bf16[2,128,128]{2,1,0:T(8,128)(2,1)S(1)} %collective-permute-done.9, f32[8,128,128]{2,1,0:T(8,128)S(1)} %get-tuple-element.44, bf16[8,128,128]{2,1,0:T(8,128)(2,1)} %collective-permute-done.7), kind=kLoop, calls=%fused_computation.5 | loop fusion | flops 163840 | bytes 327680 | tf_op jit(solution)/shard_map/convert_element_type | solution.py:357
  37.3 2.7 %collective-permute-start.10 = (bf16[2,128,128]{2,1,0:T(8,128)(2,1)S(1)}, bf16[2,128,128]{2,1,0:T(8,128)(2,1)S(1)}, u32[]{:S(2)}, u32[]{:S(2)}) collective-permute-start(bf16[2,128,128]{2,1,0:T(8,128)(2,1)S(1)} %add_convert_fusion.3), channel_id=1, source_target_pairs={{0,4},{1,5},{2,6},{3,7},{4,0},{5,1},{6,2},{7,3},{8,12},{9,13},{10,... | collective-permute-start | bytes 196616 | tf_op jit(solution)/shard_map/ppermute | solution.py:308
  40.0 1.8 %collective-permute-done.12 = bf16[6,128,128]{2,1,0:T(8,128)(2,1)S(1)} collective-permute-done((bf16[6,128,128]{2,1,0:T(8,128)(2,1)S(1)}, bf16[6,128,128]{2,1,0:T(8,128)(2,1)S(1)}, u32[]{:S(2)}, u32[]{:S(2)}) %collective-permute-start.12) | collective-permute-done | bytes 196640 | tf_op jit(solution)/shard_map/ppermute | solution.py:308
  41.8 1.0 %add_convert_fusion.1 = bf16[6,128,128]{2,1,0:T(8,128)(2,1)S(1)} fusion(bf16[6,128,128]{2,1,0:T(8,128)(2,1)S(1)} %collective-permute-done.12, f32[8,128,128]{2,1,0:T(8,128)S(1)} %get-tuple-element.44, bf16[8,128,128]{2,1,0:T(8,128)(2,1)} %collective-permute-done.7), kind=kLoop, calls=%fused_computation.3 | loop fusion | flops 491520 | bytes 983040 | tf_op jit(solution)/shard_map/convert_element_type | solution.py:357
  42.8 2.0 %collective-permute-start.13 = (bf16[6,128,128]{2,1,0:T(8,128)(2,1)S(1)}, bf16[6,128,128]{2,1,0:T(8,128)(2,1)S(1)}, u32[]{:S(2)}, u32[]{:S(2)}) collective-permute-start(bf16[6,128,128]{2,1,0:T(8,128)(2,1)S(1)} %add_convert_fusion.1), channel_id=1, source_target_pairs={{0,4},{1,5},{2,6},{3,7},{4,0},{5,1},{6,2},{7,3},{8,12},{9,13},{10,... | collective-permute-start | bytes 589832 | tf_op jit(solution)/shard_map/ppermute | solution.py:308
  44.8 5.5 %collective-permute-done.6 = bf16[8,128,128]{2,1,0:T(8,128)(2,1)S(1)} collective-permute-done((bf16[8,128,128]{2,1,0:T(8,128)(2,1)S(1)}, bf16[8,128,128]{2,1,0:T(8,128)(2,1)S(1)}, u32[]{:S(2)}, u32[]{:S(2)}) %collective-permute-start.6) | collective-permute-done | bytes 262176 | tf_op jit(solution)/shard_map/ppermute | solution.py:308
  50.2 1.0 %convert_add_fusion = f32[8,128,128]{2,1,0:T(8,128)S(1)} fusion(bf16[8,128,128]{2,1,0:T(8,128)(2,1)S(1)} %collective-permute-done.6, f32[8,128,128]{2,1,0:T(8,128)S(1)} %get-tuple-element.40, bf16[8,128,128]{2,1,0:T(8,128)(2,1)} %collective-permute-done.4), kind=kLoop, calls=%fused_computation.1 | loop fusion | flops 524288 | bytes 1572864 | tf_op jit(solution)/shard_map/add | solution.py:362
  51.3 3.7 %collective-permute-done.13 = bf16[6,128,128]{2,1,0:T(8,128)(2,1)S(1)} collective-permute-done((bf16[6,128,128]{2,1,0:T(8,128)(2,1)S(1)}, bf16[6,128,128]{2,1,0:T(8,128)(2,1)S(1)}, u32[]{:S(2)}, u32[]{:S(2)}) %collective-permute-start.13) | collective-permute-done | bytes 196640 | tf_op jit(solution)/shard_map/ppermute | solution.py:308
  55.0 0.9 %multiply_bitcast_fusion = f32[1,8,128,128]{3,2,1,0:T(8,128)} fusion(f32[8,128,128]{2,1,0:T(8,128)S(1)} %convert_add_fusion, bf16[6,128,128]{2,1,0:T(8,128)(2,1)S(1)} %collective-permute-done.13, bf16[2,128,128]{2,1,0:T(8,128)(2,1)S(1)} %collective-permute-done.10), kind=kLoop, calls=%fused_computation | loop fusion | flops 524288 | bytes 1310720 | tf_op jit(solution)/shard_map/broadcast_in_dim | solution.py:372
  (25 shorter events, 3.7 us)
Async XLA Ops:
  5.5 13.5 %copy-start.1 = (bf16[1,64,4096]{2,1,0:T(8,128)(2,1)S(1)}, bf16[1,64,4096]{2,1,0:T(8,128)(2,1)}, u32[]{:S(2)}) copy-start(bf16[1,64,4096]{2,1,0:T(8,128)(2,1)} %param.9) | copy-start | bytes 1572868
  5.5 13.5 %copy-start.2 = (s32[1,4,16]{2,1,0:T(4,128)S(1)}, s32[1,4,16]{2,1,0:T(4,128)}, u32[]{:S(2)}) copy-start(s32[1,4,16]{2,1,0:T(4,128)} %param.13) | copy-start | bytes 772
  5.5 9.5 %collective-permute-start.1 = (bf16[64,1024]{1,0:T(8,128)(2,1)S(1)}, bf16[64,1024]{1,0:T(8,128)(2,1)S(1)}, u32[]{:S(2)}, u32[]{:S(2)}) collective-permute-start(bf16[64,1024]{1,0:T(8,128)(2,1)S(1)} %get-tuple-element.33), channel_id=1, source_target_pairs={{0,24},{8,0},{16,8},{24,16},{1,25},{9,1},{17,9},{25,17},{2,26},{10... | collective-permute-start | bytes 393224 | tf_op jit(solution)/shard_map/ppermute | solution.py:313
  9.5 6.7 %collective-permute-start.2 = (bf16[64,1024]{1,0:T(8,128)(2,1)S(1)}, bf16[64,1024]{1,0:T(8,128)(2,1)S(1)}, u32[]{:S(2)}, u32[]{:S(2)}) collective-permute-start(bf16[64,1024]{1,0:T(8,128)(2,1)S(1)} %get-tuple-element.34), channel_id=1, source_target_pairs={{0,24},{8,0},{16,8},{24,16},{1,25},{9,1},{17,9},{25,17},{2,26},{10... | collective-permute-start | bytes 393224 | tf_op jit(solution)/shard_map/ppermute | solution.py:313
  10.0 9.0 %collective-permute-start = (bf16[64,1024]{1,0:T(8,128)(2,1)S(1)}, bf16[64,1024]{1,0:T(8,128)(2,1)S(1)}, u32[]{:S(2)}, u32[]{:S(2)}) collective-permute-start(bf16[64,1024]{1,0:T(8,128)(2,1)S(1)} %get-tuple-element.28), channel_id=1, source_target_pairs={{0,24},{8,0},{16,8},{24,16},{1,25},{9,1},{17,9},{25,17},{2,26},{10... | collective-permute-start | bytes 393224 | tf_op jit(solution)/shard_map/ppermute | solution.py:313
  11.4 9.2 %collective-permute-start.3 = (bf16[64,1024]{1,0:T(8,128)(2,1)S(1)}, bf16[64,1024]{1,0:T(8,128)(2,1)S(1)}, u32[]{:S(2)}, u32[]{:S(2)}) collective-permute-start(bf16[64,1024]{1,0:T(8,128)(2,1)S(1)} %get-tuple-element.38), channel_id=1, source_target_pairs={{0,24},{8,0},{16,8},{24,16},{1,25},{9,1},{17,9},{25,17},{2,26},{10... | collective-permute-start | bytes 393224 | tf_op jit(solution)/shard_map/ppermute | solution.py:313
  21.6 2.0 %copy-start = (bf16[128,4096]{1,0:T(8,128)(2,1)}, bf16[128,4096]{1,0:T(8,128)(2,1)S(1)}, u32[]{:S(2)}) copy-start(bf16[128,4096]{1,0:T(8,128)(2,1)S(1)} %get-tuple-element.39.stack) | copy-start | bytes 3145732
  21.6 8.2 %collective-permute-start.8 = (bf16[2,128,128]{2,1,0:T(8,128)(2,1)S(1)}, bf16[2,128,128]{2,1,0:T(8,128)(2,1)}, u32[]{:S(2)}, u32[]{:S(2)}) collective-permute-start(bf16[2,128,128]{2,1,0:T(8,128)(2,1)S(1)} %get-tuple-element.47), channel_id=1, source_target_pairs={{0,1},{1,0},{2,3},{3,2},{4,5},{5,4},{6,7},{7,6},{8,9},{9,8},{10,11... | collective-permute-start | bytes 196616 | tf_op jit(solution)/shard_map/ppermute | solution.py:308
  21.6 10.7 %collective-permute-start.11 = (bf16[6,128,128]{2,1,0:T(8,128)(2,1)}, bf16[6,128,128]{2,1,0:T(8,128)(2,1)}, u32[]{:S(2)}, u32[]{:S(2)}) collective-permute-start(bf16[6,128,128]{2,1,0:T(8,128)(2,1)} %get-tuple-element.48), channel_id=1, source_target_pairs={{0,1},{1,0},{2,3},{3,2},{4,5},{5,4},{6,7},{7,6},{8,9},{9,8},{10,11... | collective-permute-start | bytes 589832 | tf_op jit(solution)/shard_map/ppermute | solution.py:308
  22.4 14.0 %collective-permute-start.7 = (bf16[8,128,128]{2,1,0:T(8,128)(2,1)S(1)}, bf16[8,128,128]{2,1,0:T(8,128)(2,1)}, u32[]{:S(2)}, u32[]{:S(2)}) collective-permute-start(bf16[8,128,128]{2,1,0:T(8,128)(2,1)S(1)} %get-tuple-element.45), channel_id=1, source_target_pairs={{0,1},{1,0},{2,3},{3,2},{4,5},{5,4},{6,7},{7,6},{8,9},{9,8},{10,11... | collective-permute-start | bytes 786440 | tf_op jit(solution)/shard_map/ppermute | solution.py:308
  23.0 10.8 %collective-permute-start.5 = (bf16[8,128,128]{2,1,0:T(8,128)(2,1)S(1)}, bf16[8,128,128]{2,1,0:T(8,128)(2,1)}, u32[]{:S(2)}, u32[]{:S(2)}) collective-permute-start(bf16[8,128,128]{2,1,0:T(8,128)(2,1)S(1)} %get-tuple-element.43), channel_id=1, source_target_pairs={{0,1},{1,0},{2,3},{3,2},{4,5},{5,4},{6,7},{7,6},{8,9},{9,8},{10,11... | collective-permute-start | bytes 786440 | tf_op jit(solution)/shard_map/ppermute | solution.py:308
  23.5 21.2 %collective-permute-start.4 = (bf16[8,128,128]{2,1,0:T(8,128)(2,1)S(1)}, bf16[8,128,128]{2,1,0:T(8,128)(2,1)}, u32[]{:S(2)}, u32[]{:S(2)}) collective-permute-start(bf16[8,128,128]{2,1,0:T(8,128)(2,1)S(1)} %get-tuple-element.41), channel_id=1, source_target_pairs={{0,1},{1,0},{2,3},{3,2},{4,5},{5,4},{6,7},{7,6},{8,9},{9,8},{10,11... | collective-permute-start | bytes 786440 | tf_op jit(solution)/shard_map/ppermute | solution.py:308
  30.6 5.8 %collective-permute-start.9 = (bf16[2,128,128]{2,1,0:T(8,128)(2,1)S(1)}, bf16[2,128,128]{2,1,0:T(8,128)(2,1)S(1)}, u32[]{:S(2)}, u32[]{:S(2)}) collective-permute-start(bf16[2,128,128]{2,1,0:T(8,128)(2,1)S(1)} %add_convert_fusion.4), channel_id=1, source_target_pairs={{0,2},{1,3},{2,0},{3,1},{4,6},{5,7},{6,4},{7,5},{8,10},{9,11},{10,... | collective-permute-start | bytes 196616 | tf_op jit(solution)/shard_map/ppermute | solution.py:308
  33.3 8.5 %collective-permute-start.12 = (bf16[6,128,128]{2,1,0:T(8,128)(2,1)S(1)}, bf16[6,128,128]{2,1,0:T(8,128)(2,1)S(1)}, u32[]{:S(2)}, u32[]{:S(2)}) collective-permute-start(bf16[6,128,128]{2,1,0:T(8,128)(2,1)S(1)} %add_convert_fusion.2), channel_id=1, source_target_pairs={{0,2},{1,3},{2,0},{3,1},{4,6},{5,7},{6,4},{7,5},{8,10},{9,11},{10,... | collective-permute-start | bytes 589832 | tf_op jit(solution)/shard_map/ppermute | solution.py:308
  34.8 15.5 %collective-permute-start.6 = (bf16[8,128,128]{2,1,0:T(8,128)(2,1)S(1)}, bf16[8,128,128]{2,1,0:T(8,128)(2,1)S(1)}, u32[]{:S(2)}, u32[]{:S(2)}) collective-permute-start(bf16[8,128,128]{2,1,0:T(8,128)(2,1)S(1)} %add_convert_fusion), channel_id=1, source_target_pairs={{0,2},{1,3},{2,0},{3,1},{4,6},{5,7},{6,4},{7,5},{8,10},{9,11},{10,... | collective-permute-start | bytes 786440 | tf_op jit(solution)/shard_map/ppermute | solution.py:308
  37.3 13.9 %collective-permute-start.10 = (bf16[2,128,128]{2,1,0:T(8,128)(2,1)S(1)}, bf16[2,128,128]{2,1,0:T(8,128)(2,1)S(1)}, u32[]{:S(2)}, u32[]{:S(2)}) collective-permute-start(bf16[2,128,128]{2,1,0:T(8,128)(2,1)S(1)} %add_convert_fusion.3), channel_id=1, source_target_pairs={{0,4},{1,5},{2,6},{3,7},{4,0},{5,1},{6,2},{7,3},{8,12},{9,13},{10,... | collective-permute-start | bytes 196616 | tf_op jit(solution)/shard_map/ppermute | solution.py:308
  42.8 12.1 %collective-permute-start.13 = (bf16[6,128,128]{2,1,0:T(8,128)(2,1)S(1)}, bf16[6,128,128]{2,1,0:T(8,128)(2,1)S(1)}, u32[]{:S(2)}, u32[]{:S(2)}) collective-permute-start(bf16[6,128,128]{2,1,0:T(8,128)(2,1)S(1)} %add_convert_fusion.1), channel_id=1, source_target_pairs={{0,4},{1,5},{2,6},{3,7},{4,0},{5,1},{6,2},{7,3},{8,12},{9,13},{10,... | collective-permute-start | bytes 589832 | tf_op jit(solution)/shard_map/ppermute | solution.py:308
